TPU v7x, 32 devices: a whole 2x2x4 slice. The times are simulated.
32 devices in a mesh: dp: 16 (over z, y, x), tensor: 2 (over core).
Axes of the slice: x: 2, y: 2, z: 4, core: 2. Of those that a mesh axis runs over, the one named last changes fastest.
Arguments:
- layer_input: bfloat16 [32, 1024, 768], P(('dp', 'tensor')), may hold values from -6 to 6
- lengths: int32 [32], P('dp'), may hold values from 100 to 1024, as said below
- predicted: int32 [32, 1024], P(('dp', 'tensor')), may hold values from 0 to 69
- w_qkv: bfloat16 [3, 768, 768], P(None, None, 'tensor'), may hold values from -0.21875 to 0.21875
- b_qkv: bfloat16 [3, 768], P(None, 'tensor'), may hold values from -3 to 3
- w_out: bfloat16 [768, 768], P('tensor'), may hold values from -1.75 to 1.75
- b_out: bfloat16 [768], replicated, may hold values from -2 to 2
- w_up: bfloat16 [768, 3072], P(None, 'tensor'), may hold values from -0.21875 to 0.21875
- b_up: bfloat16 [3072], P('tensor'), may hold values from -3 to 3
- w_down: bfloat16 [3072, 768], P('tensor'), may hold values from -0.109375 to 0.109375
- b_down: bfloat16 [768], replicated, may hold values from -2 to 2
- first_gain: bfloat16 [768], replicated, may hold values from 0.099609375 to 1.8984375
- first_bias: bfloat16 [768], replicated, may hold values from -2 to 2
- second_gain: bfloat16 [768], replicated, may hold values from 0.099609375 to 1.8984375
- second_bias: bfloat16 [768], replicated, may hold values from -2 to 2
- cotangent: bfloat16 [32, 1024, 768], P(('dp', 'tensor')), may hold values from -6 to 6
Outputs:
- layer_output: bfloat16 [32, 1024, 768], P(('dp', 'tensor'))
- input_grad: bfloat16 [32, 1024, 768], P(('dp', 'tensor'))
- grad_w_qkv: float32 [3, 768, 768], P(None, None, 'tensor')
- grad_b_qkv: float32 [3, 768], P(None, 'tensor')
- grad_w_out: float32 [768, 768], P('tensor')
- grad_b_out: float32 [768], replicated
- grad_w_up: float32 [768, 3072], P(None, 'tensor')
- grad_b_up: float32 [3072], P('tensor')
- grad_w_down: float32 [3072, 768], P('tensor')
- grad_b_down: float32 [768], replicated
- grad_first_gain: float32 [768], replicated
- grad_first_bias: float32 [768], replicated
- grad_second_gain: float32 [768], replicated
- grad_second_bias: float32 [768], replicated
- codon_rate: float32 [70], replicated
Inputs may be any that keep to these rules, and one draw needn't show every extreme that they name: `lengths`: a sequence holds its real codons at positions below its length and padding after; the first sequence has 1024 codons. `predicted`: padded positions hold classes as well.
All inputs are finite; a program needn't handle non-finite values.
Results may differ from a plain program's by a relative error of at most 0.015.
Values may be sent and summed in bfloat16 or wider, within the bound.
No kernel may reach another device: no remote copies, remote signals or barrier semaphores. Data moves between devices by JAX's collectives and lax.ppermute only.
A program may use at most 256 MiB of HBM per device.

v0:
```python
from functools import partial

import jax
import jax.numpy as jnp
from jax import lax
from jax.sharding import PartitionSpec as P

HEAD_DIM = 64
CLASSES = 70


EPSILON = 1e-05


def norm_layer(inputs, gain_vec, shift_vec):
    row_mean = jnp.mean(inputs, axis=-1, keepdims=True)
    centred = inputs - row_mean
    variance = jnp.mean(centred * centred, axis=-1, keepdims=True)
    return centred * lax.rsqrt(variance + EPSILON) * gain_vec + shift_vec


def rotary_tables(seq_len, head_size):
    half_dim = head_size // 2
    frequency = 10000.0 ** (-2.0 * jnp.arange(half_dim).astype(jnp.float32) / head_size)
    angles = jnp.arange(seq_len).astype(jnp.float32)[:, None] * frequency[None, :]
    angles = jnp.concatenate([angles, angles], axis=1)
    return (jnp.cos(angles), jnp.sin(angles))


def rotate(inputs, cosine_table, sine_table):
    half_dim = inputs.shape[-1] // 2
    turned = jnp.concatenate([-inputs[..., half_dim:], inputs[..., :half_dim]], axis=-1)
    return inputs * cosine_table[:, None, :] + turned * sine_table[:, None, :]


def gelu_exact(inputs):
    return jax.nn.gelu(inputs, approximate=False)


def masked_scores(queries, keys_rot, key_valid, score_scale):
    scores = (
        jnp.einsum("qhd,khd->hqk", queries, keys_rot, preferred_element_type=jnp.float32)
        * score_scale
    )
    return jnp.where(key_valid[None, None, :], scores, -1000000000.0)


def attend_forward(pieces, score_scale):
    queries, keys_rot, values, key_valid = pieces
    scores = masked_scores(queries, keys_rot, key_valid, score_scale)
    row_top = jnp.max(scores, axis=-1, keepdims=True)
    row_total = jnp.sum(jnp.exp(scores - row_top), axis=-1, keepdims=True)
    log_total = row_top + jnp.log(row_total)
    prob_low = jnp.exp(scores - log_total).astype(jnp.bfloat16)
    mixed_heads = jnp.einsum("hqk,khd->qhd", prob_low, values, preferred_element_type=jnp.float32)
    return (mixed_heads.astype(jnp.bfloat16), log_total)


def attend_backward(pieces, score_scale):
    queries, keys_rot, values, key_valid, log_total, grad_mixed = pieces
    scores = masked_scores(queries, keys_rot, key_valid, score_scale)
    prob_full = jnp.exp(scores - log_total)
    prob_low = prob_full.astype(jnp.bfloat16)
    grad_values = jnp.einsum(
        "hqk,qhd->khd", prob_low, grad_mixed, preferred_element_type=jnp.float32
    )
    grad_probs = jnp.einsum("qhd,khd->hqk", grad_mixed, values, preferred_element_type=jnp.float32)
    row_delta = jnp.sum(prob_full * grad_probs, axis=-1, keepdims=True)
    grad_scores = (prob_full * (grad_probs - row_delta)).astype(jnp.bfloat16)
    grad_queries = (
        jnp.einsum("hqk,khd->qhd", grad_scores, keys_rot, preferred_element_type=jnp.float32)
        * score_scale
    )
    grad_keys = (
        jnp.einsum("hqk,qhd->khd", grad_scores, queries, preferred_element_type=jnp.float32)
        * score_scale
    )
    return (grad_queries, grad_keys, grad_values)


def per_device(
    layer_input,
    lengths,
    predicted,
    w_qkv,
    b_qkv,
    w_out,
    b_out,
    w_up,
    b_up,
    w_down,
    b_down,
    first_gain,
    first_bias,
    second_gain,
    second_bias,
    cotangent,
):
    own_seqs, length, model_width = layer_input.shape
    slices = lax.axis_size("tensor")
    local_width = w_out.shape[0]
    local_heads = local_width // HEAD_DIM
    all_seqs = own_seqs * slices
    score_scale = HEAD_DIM ** (-0.5)
    cosine_table, sine_table = rotary_tables(length, HEAD_DIM)
    positions = jnp.arange(length)
    group_valid = positions[None, :] < lengths[:, None]
    own_lengths = lax.dynamic_slice_in_dim(
        lengths, lax.axis_index("tensor") * own_seqs, own_seqs, 0
    )
    own_valid = positions[None, :] < own_lengths[:, None]
    residual_in = layer_input.astype(jnp.float32)
    normed_one, norm_one_pull = jax.vjp(
        norm_layer, residual_in, first_gain.astype(jnp.float32), first_bias.astype(jnp.float32)
    )
    joined_one = lax.all_gather(normed_one.astype(jnp.bfloat16), "tensor", axis=0, tiled=True)
    projected = jnp.einsum("gld,cde->cgle", joined_one, w_qkv, preferred_element_type=jnp.float32)
    projected = projected + b_qkv.astype(jnp.float32)[:, None, None, :]
    shaped = projected.reshape(3, all_seqs, length, local_heads, HEAD_DIM)
    rotated, rope_pull = jax.vjp(
        lambda first_part, second_part: (
            rotate(first_part, cosine_table, sine_table),
            rotate(second_part, cosine_table, sine_table),
        ),
        shaped[0],
        shaped[1],
    )
    queries = rotated[0].astype(jnp.bfloat16)
    keys_rot = rotated[1].astype(jnp.bfloat16)
    values = shaped[2].astype(jnp.bfloat16)
    mixed_heads, log_total = lax.map(
        partial(attend_forward, score_scale=score_scale), (queries, keys_rot, values, group_valid)
    )
    mixed_flat = mixed_heads.reshape(all_seqs, length, local_width)
    picked = mixed_flat
    attention = lax.psum_scatter(
        jnp.einsum("gle,ed->gld", picked, w_out, preferred_element_type=jnp.float32).astype(
            jnp.bfloat16
        ),
        "tensor",
        scatter_dimension=0,
        tiled=True,
    ).astype(jnp.float32) + b_out.astype(jnp.float32)
    residual = residual_in + attention
    normed_two, norm_two_pull = jax.vjp(
        norm_layer, residual, second_gain.astype(jnp.float32), second_bias.astype(jnp.float32)
    )
    joined_two = lax.all_gather(normed_two.astype(jnp.bfloat16), "tensor", axis=0, tiled=True)
    up_proj = jnp.einsum("gld,df->glf", joined_two, w_up, preferred_element_type=jnp.float32)
    up_proj = up_proj + b_up.astype(jnp.float32)
    activation, gelu_pull = jax.vjp(gelu_exact, up_proj)
    act_low = activation.astype(jnp.bfloat16)
    picked = act_low
    feed_forward = lax.psum_scatter(
        jnp.einsum("glf,fd->gld", picked, w_down, preferred_element_type=jnp.float32).astype(
            jnp.bfloat16
        ),
        "tensor",
        scatter_dimension=0,
        tiled=True,
    ).astype(jnp.float32) + b_down.astype(jnp.float32)
    layer_output = (residual + feed_forward).astype(jnp.bfloat16)
    grad_output = cotangent.astype(jnp.float32)
    grad_b_down = jnp.sum(grad_output, axis=(0, 1))
    grad_joined = lax.all_gather(cotangent, "tensor", axis=0, tiled=True)
    grad_w_down = jnp.einsum(
        "glf,gld->fd", act_low, grad_joined, preferred_element_type=jnp.float32
    )
    grad_act = jnp.einsum("gld,fd->glf", grad_joined, w_down, preferred_element_type=jnp.float32)
    grad_up = gelu_pull(grad_act)[0].astype(jnp.bfloat16)
    grad_b_up = jnp.sum(grad_up, axis=(0, 1), dtype=jnp.float32)
    grad_w_up = jnp.einsum("gld,glf->df", joined_two, grad_up, preferred_element_type=jnp.float32)
    picked = grad_up
    grad_normed_two = lax.psum_scatter(
        jnp.einsum("glf,df->gld", picked, w_up, preferred_element_type=jnp.float32).astype(
            jnp.bfloat16
        ),
        "tensor",
        scatter_dimension=0,
        tiled=True,
    ).astype(jnp.float32)
    grad_res_part, grad_second_gain, grad_second_bias = norm_two_pull(grad_normed_two)
    grad_residual = grad_output + grad_res_part
    grad_attention = grad_residual.astype(jnp.bfloat16)
    grad_b_out = jnp.sum(grad_attention, axis=(0, 1), dtype=jnp.float32)
    attn_joined = lax.all_gather(grad_attention, "tensor", axis=0, tiled=True)
    grad_w_out = jnp.einsum(
        "gle,gld->ed", mixed_flat, attn_joined, preferred_element_type=jnp.float32
    )
    grad_mixed = jnp.einsum("gld,ed->gle", attn_joined, w_out, preferred_element_type=jnp.float32)
    grad_mixed = grad_mixed.astype(jnp.bfloat16).reshape(all_seqs, length, local_heads, HEAD_DIM)
    grad_queries, grad_keys, grad_values = lax.map(
        partial(attend_backward, score_scale=score_scale),
        (queries, keys_rot, values, group_valid, log_total, grad_mixed),
    )
    grad_q_lin, grad_k_lin = rope_pull((grad_queries, grad_keys))
    grad_qkv = jnp.stack([grad_q_lin, grad_k_lin, grad_values]).reshape(
        3, all_seqs, length, local_width
    )
    grad_qkv = grad_qkv.astype(jnp.bfloat16)
    grad_b_qkv = jnp.sum(grad_qkv, axis=(1, 2), dtype=jnp.float32)
    grad_w_qkv = jnp.einsum(
        "gld,cgle->cde", joined_one, grad_qkv, preferred_element_type=jnp.float32
    )
    picked = grad_qkv
    grad_normed_one = lax.psum_scatter(
        jnp.einsum("cgle,cde->gld", picked, w_qkv, preferred_element_type=jnp.float32).astype(
            jnp.bfloat16
        ),
        "tensor",
        scatter_dimension=0,
        tiled=True,
    ).astype(jnp.float32)
    grad_in_part, grad_first_gain, grad_first_bias = norm_one_pull(grad_normed_one)
    input_grad = (grad_residual + grad_in_part).astype(jnp.bfloat16)
    classes = jnp.arange(CLASSES)
    class_hits = jnp.where(
        (predicted[None, :, :] == classes[:, None, None]) & own_valid[None, :, :],
        jnp.float32(1.0),
        jnp.float32(0.0),
    )
    class_counts = jnp.sum(class_hits, axis=(1, 2))
    (
        grad_first_gain,
        grad_first_bias,
        grad_second_gain,
        grad_second_bias,
        grad_b_out,
        grad_b_down,
        class_counts,
    ) = lax.psum(
        (
            grad_first_gain,
            grad_first_bias,
            grad_second_gain,
            grad_second_bias,
            grad_b_out,
            grad_b_down,
            class_counts,
        ),
        ("dp", "tensor"),
    )
    grad_w_qkv, grad_b_qkv, grad_w_out, grad_w_up, grad_b_up, grad_w_down = lax.psum(
        (grad_w_qkv, grad_b_qkv, grad_w_out, grad_w_up, grad_b_up, grad_w_down), "dp"
    )
    total_tokens = own_seqs * length * slices * lax.axis_size("dp")
    codon_rate = class_counts * (CLASSES / total_tokens)
    return (
        layer_output,
        input_grad,
        grad_w_qkv,
        grad_b_qkv,
        grad_w_out,
        grad_b_out,
        grad_w_up,
        grad_b_up,
        grad_w_down,
        grad_b_down,
        grad_first_gain,
        grad_first_bias,
        grad_second_gain,
        grad_second_bias,
        codon_rate,
    )


def solution(mesh):
    placed = (
        P(("dp", "tensor"), None, None),
        P("dp"),
        P(("dp", "tensor"), None),
        P(None, None, "tensor"),
        P(None, "tensor"),
        P("tensor", None),
        P(),
        P(None, "tensor"),
        P("tensor"),
        P("tensor", None),
        P(),
        P(),
        P(),
        P(),
        P(),
        P(("dp", "tensor"), None, None),
    )
    return jax.shard_map(
        per_device,
        mesh=mesh,
        in_specs=placed,
        out_specs=(
            P(("dp", "tensor"), None, None),
            P(("dp", "tensor"), None, None),
            P(None, None, "tensor"),
            P(None, "tensor"),
            P("tensor", None),
            P(),
            P(None, "tensor"),
            P("tensor"),
            P("tensor", None),
            P(),
            P(),
            P(),
            P(),
            P(),
            P(),
        ),
        check_vma=False,
    )
```

profile of v0, /device:TPU:0, one launch (start us, length us, event | category | flops | bytes accessed | tf_op | source)
XLA Modules:
  0.0 917.4 jit_solution(5525578141528651944)
XLA Ops:
  16.9 13.7 %all-gather.5.cloned.1.call-done = bf16[2,1024,768]{2,1,0:T(8,128)(2,1)} async-done(((bf16[1,1024,768]{2,1,0:T(8,128)(2,1)}), bf16[2,1024,768]{2,1,0:T(8,128)(2,1)}) %all-gather.5.cloned.1.call-update) | async-done | bytes 3145744 | tf_op jit(solution)/shard_map/all_gather | solution.py:116
  30.6 6.5 add_bitcast_fusion
  44.0 72.6 %while.26 = (s32[]{:T(128)}, bf16[2,1024,6,64]{1,3,2,0:T(8,128)(2,1)}, f32[2,6,1024,1]{2,1,3,0:T(8,128)S(1)}, bf16[2,1024,6,64]{1,3,2,0:T(8,128)(2,1)}, pred[2,1...) while((s32[]{:T(128)}, ...), condition=%wide.region_5.6_spmd, body=%wide.region_2.5_spmd.sunk | while | flops 1680205824 | bytes 97762480 | solution.py:131
  44.3 11.9 %fusion.141 = (f32[6,1024]{1,0:T(8,128)S(1)}, f32[6,1024,1024]{1,2,0:T(8,128)}) fusion(pred[1024]{0:T(1024)(128)(4,1)S(1)} %dynamic-slice_reduce_fusion.4, bf16[2,1024,6,64]{1,3,2,0:T(8,128)(2,1)} %get-tuple-element.404, s32[]{:T(128)S(6)} %copy.103, bf16[2,1024,6,64]{1,3,2,0:T(8,128)(2,1)} %get-tuple-element.403), kind=kOutput, calls=%fused_computation.3.clone.1 | convolution fusion | flops 824174592 | bytes 26765312 | tf_op jit(solution)/shard_map/while/body/eval_jaxpr/qhd,khd->hqk/dot_general | solution.py:42
  56.2 11.8 %exponential_reduce_fusion.2 = f32[6,1024]{1,0:T(8,128)S(1)} fusion(f32[6,1024,1024]{1,2,0:T(8,128)} %get-tuple-element.366, f32[6,1024]{1,0:T(8,128)S(1)} %get-tuple-element.367, pred[1024]{0:T(1024)(128)(4,1)S(1)} %dynamic-slice_reduce_fusion.4), kind=kLoop, calls=%fused_computation.1.clone.1 | loop fusion | flops 25159680 | bytes 25216000 | tf_op jit(solution)/shard_map/while/body/eval_jaxpr/reduce_sum | solution.py:52
  68.1 11.2 %fusion.142 = bf16[2,1024,6,64]{1,3,2,0:T(8,128)(2,1)S(1)} fusion(bf16[2,1024,6,64]{1,3,2,0:T(8,128)(2,1)S(1)} %copy-done.59, s32[]{:T(128)S(6)} %copy.103, f32[6,1024,1024]{1,2,0:T(8,128)} %get-tuple-element.366, f32[6,1024]{1,0:T(8,128)S(1)} %get-tuple-element.368, pred[1024]{0:T(1024)(128)(4,1)S(1)} %dynamic-slice_reduce_fusion.4, ...), kind=kOutput, calls=%fused_computation.8.clone.1 | convolution fusion | flops 830865408 | bytes 26773504 | tf_op jit(solution)/shard_map/while/body/eval_jaxpr/hqk,khd->qhd/dot_general | solution.py:55
  80.5 11.9 %fusion.141 = (f32[6,1024]{1,0:T(8,128)S(1)}, f32[6,1024,1024]{1,2,0:T(8,128)}) fusion(pred[1024]{0:T(1024)(128)(4,1)S(1)} %dynamic-slice_reduce_fusion.4, bf16[2,1024,6,64]{1,3,2,0:T(8,128)(2,1)} %get-tuple-element.404, s32[]{:T(128)S(6)} %copy.103, bf16[2,1024,6,64]{1,3,2,0:T(8,128)(2,1)} %get-tuple-element.403), kind=kOutput, calls=%fused_computation.3.clone.1 | convolution fusion | flops 824174592 | bytes 26765312 | tf_op jit(solution)/shard_map/while/body/eval_jaxpr/qhd,khd->hqk/dot_general | solution.py:42
  92.4 11.8 %exponential_reduce_fusion.2 = f32[6,1024]{1,0:T(8,128)S(1)} fusion(f32[6,1024,1024]{1,2,0:T(8,128)} %get-tuple-element.366, f32[6,1024]{1,0:T(8,128)S(1)} %get-tuple-element.367, pred[1024]{0:T(1024)(128)(4,1)S(1)} %dynamic-slice_reduce_fusion.4), kind=kLoop, calls=%fused_computation.1.clone.1 | loop fusion | flops 25159680 | bytes 25216000 | tf_op jit(solution)/shard_map/while/body/eval_jaxpr/reduce_sum | solution.py:52
  104.3 11.2 %fusion.142 = bf16[2,1024,6,64]{1,3,2,0:T(8,128)(2,1)S(1)} fusion(bf16[2,1024,6,64]{1,3,2,0:T(8,128)(2,1)S(1)} %copy-done.59, s32[]{:T(128)S(6)} %copy.103, f32[6,1024,1024]{1,2,0:T(8,128)} %get-tuple-element.366, f32[6,1024]{1,0:T(8,128)S(1)} %get-tuple-element.368, pred[1024]{0:T(1024)(128)(4,1)S(1)} %dynamic-slice_reduce_fusion.4, ...), kind=kOutput, calls=%fused_computation.8.clone.1 | convolution fusion | flops 830865408 | bytes 26773504 | tf_op jit(solution)/shard_map/while/body/eval_jaxpr/hqk,khd->qhd/dot_general | solution.py:55
  116.6 4.9 convolution_convert_fusion
  121.7 12.4 %reduce-scatter.5.cloned.1.call-done = bf16[1,1024,768]{2,1,0:T(8,128)(2,1)} async-done(((bf16[2,1024,768]{2,1,0:T(8,128)(2,1)}), bf16[1,1024,768]{2,1,0:T(8,128)(2,1)}) %reduce-scatter.5.cloned.1.call-update) | async-done | bytes 1572880 | tf_op jit(solution)/shard_map/reduce_scatter | solution.py:136
  141.0 12.4 %all-gather.7.cloned.1.call-done = bf16[2,1024,768]{2,1,0:T(8,128)(2,1)} async-done(((bf16[1,1024,768]{2,1,0:T(8,128)(2,1)}), bf16[2,1024,768]{2,1,0:T(8,128)(2,1)}) %all-gather.7.cloned.1.call-update) | async-done | bytes 3145744 | tf_op jit(solution)/shard_map/all_gather | solution.py:148
  153.4 10.8 %fusion.78 = (u8[1024,1536]{1,0:T(8,128)(4,1)S(1)}, u8[1024,1536]{1,0:T(8,128)(4,1)S(1)}, f32[2,1024,1536]{2,1,0:T(8,128)S(1)}) fusion(f32[1536]{0:T(1024)S(1)} %convert_element_type.147, bf16[2,1024,768]{2,1,0:T(8,128)(2,1)} %all-gather.7.cloned.1.call-done, bf16[768,1536]{1,0:T(8,128)(2,1)S(1)} %copy-done), kind=kOutput, calls=%fused_computation.132 | convolution fusion | flops 4872732672 | bytes 21239808 | tf_op jit(solution)/shard_map/gld,df->glf/dot_general | solution.py:149
  164.3 4.7 copy-done.15
  169.0 30.9 %multiply_convert_fusion.1 = (bf16[2,1024,1536]{2,1,0:T(8,128)(2,1)}, f32[2,1024,1536]{2,1,0:T(8,128)}) fusion(f32[2,1024,1536]{2,1,0:T(8,128)S(1)} %get-tuple-element.261, f32[1536]{0:T(1024)S(1)} %convert_element_type.147, u8[1024,1536]{1,0:T(8,128)(4,1)S(1)} %get-tuple-element.173, u8[1024,1536]{1,0:T(8,128)(4,1)S(1)} %get-tuple-element.172), kind=kLoop, calls=%fused_computation.66 | loop fusion | flops 223346688 | bytes 34609152 | tf_op jit(solution)/shard_map/convert_element_type | solution.py:152
  199.8 17.5 %convert_reduce_fusion = (f32[1536]{0:T(1024)}, bf16[2,1024,1536]{2,1,0:T(8,128)(2,1)S(1)}) fusion(f32[2,1024,1536]{2,1,0:T(8,128)} %get-tuple-element.235, bf16[2,1024,768]{2,1,0:T(8,128)(2,1)} %all-gather.9.cloned.1.call-done, bf16[1536,768]{1,0:T(8,128)(2,1)} %param.29, f32[2,1024,1536]{2,1,0:T(8,128)} %copy-done.15, f32[1536]{0:T(1024)S(1)} %convert_element_type.147), kind=kOutput, calls=%fused_computation.64 | convolution fusion | flops 4885314048 | bytes 36974592 | tf_op jit(solution)/shard_map/gld,fd->glf/dot_general | solution.py:169
  220.0 6.4 fusion.88
  228.1 9.2 %fusion.91 = bf16[2,1024,768]{2,1,0:T(8,128)(2,1)} fusion(bf16[2,1024,1536]{2,1,0:T(8,128)(2,1)} %get-tuple-element.234, bf16[1536,768]{1,0:T(8,128)(2,1)S(1)} %copy-done.57), kind=kOutput, calls=%fused_computation.143 | convolution fusion | flops 4833411072 | bytes 11796480 | tf_op jit(solution)/shard_map/glf,fd->gld/dot_general | solution.py:155
  239.0 3.8 fusion.65
  242.8 11.3 %reduce-scatter.7.cloned.1.call-done = bf16[1,1024,768]{2,1,0:T(8,128)(2,1)} async-done(((bf16[2,1024,768]{2,1,0:T(8,128)(2,1)}), bf16[1,1024,768]{2,1,0:T(8,128)(2,1)}) %reduce-scatter.7.cloned.1.call-update) | async-done | bytes 1572880 | tf_op jit(solution)/shard_map/reduce_scatter | solution.py:154
  254.1 4.6 fusion.109
  261.5 13.5 %all-gather.11.cloned.1.call-done = bf16[2,1024,768]{2,1,0:T(8,128)(2,1)} async-done(((bf16[1,1024,768]{2,1,0:T(8,128)(2,1)}), bf16[2,1024,768]{2,1,0:T(8,128)(2,1)}) %all-gather.11.cloned.1.call-update) | async-done | bytes 3145744 | tf_op jit(solution)/shard_map/all_gather | solution.py:186
  275.0 4.4 convolution_convert_fusion.1
  279.4 165.4 %while.27 = (s32[]{:T(128)}, f32[2,1024,6,64]{1,3,2,0:T(8,128)}, f32[2,1024,6,64]{1,3,2,0:T(8,128)}, bf16[2,1024,6,64]{1,3,2,0:T(8,128)(2,1)}, bf16[2,1024,6,64]...) while((s32[]{:T(128)}, f32[2,1024,6,64]{1,3,2,0:T(8,128)}, ...), condition=%wide.region_15.16_spmd, body=%wide.region_13.15_spmd.sunk | while | flops 4121683968 | bytes 262072656 | solution.py:192
  279.7 11.4 %fusion.151 = f32[6,1024,1024]{1,2,0:T(8,128)} fusion(bf16[2,1024,6,64]{1,3,2,0:T(8,128)(2,1)} %get-tuple-element.434, s32[]{:T(128)S(6)} %copy.113, bf16[2,1024,6,64]{1,3,2,0:T(8,128)(2,1)S(1)} %get-tuple-element.432), kind=kOutput, calls=%fused_computation.37.clone.1 | convolution fusion | flops 805306368 | bytes 26739712 | tf_op jit(solution)/shard_map/while/body/eval_jaxpr/qhd,khd->hqk/dot_general | solution.py:42
  291.1 12.2 %bitcast_dynamic-update-slice_fusion.11 = bf16[2,1024,6,64]{1,3,2,0:T(8,128)(2,1)} fusion(bf16[2,1024,6,64]{1,3,2,0:T(8,128)(2,1)} %get-tuple-element.420, s32[]{:T(128)S(6)} %copy.113, f32[6,1024,1024]{1,2,0:T(8,128)} %fusion.151, f32[6,1024]{1,0:T(8,128)S(1)} %dynamic-slice_bitcast_fusion.2, pred[1024]{0:T(1024)(128)(4,1)S(1)} %dynamic-slice_reduce_fusion.5, ...), kind=kOutput, calls=%fused_computation.29.clone.1 | convolution fusion | flops 830472192 | bytes 27559936 | tf_op jit(solution)/shard_map/while/body/eval_jaxpr/hqk,qhd->khd/dot_general | solution.py:64
  303.3 17.2 %multiply_reduce_fusion.3 = (f32[6,1024]{1,0:T(8,128)S(1)}, f32[6,1024,1024]{1,2,0:T(8,128)}) fusion(f32[6,1024,1024]{1,2,0:T(8,128)} %fusion.151, f32[6,1024]{1,0:T(8,128)S(1)} %dynamic-slice_bitcast_fusion.2, pred[1024]{0:T(1024)(128)(4,1)S(1)} %dynamic-slice_reduce_fusion.5, bf16[2,1024,6,64]{1,3,2,0:T(8,128)(2,1)} %get-tuple-element.437, ...), kind=kOutput, calls=%fused_computation.24.clone.1 | convolution fusion | flops 836757504 | bytes 51955712 | tf_op jit(solution)/shard_map/while/body/eval_jaxpr/qhd,khd->hqk/dot_general | solution.py:67
  320.5 23.1 %multiply_convert_fusion.3 = bf16[6,1024,1024]{1,2,0:T(8,128)(2,1)} fusion(f32[6,1024,1024]{1,2,0:T(8,128)} %get-tuple-element.380, f32[6,1024,1024]{1,2,0:T(8,128)} %fusion.151, f32[6,1024]{1,0:T(8,128)S(1)} %get-tuple-element.381, f32[6,1024]{1,0:T(8,128)S(1)} %dynamic-slice_bitcast_fusion.2, pred[1024]{0:T(1024)(128)(4,1)S(1)} %dynamic-slice_reduce_fusion.5), kind=kLoop, calls=%fused_computation.23.clone.1 | loop fusion | flops 37748736 | bytes 62964736 | tf_op jit(solution)/shard_map/while/body/eval_jaxpr/convert_element_type | solution.py:69
  343.6 8.7 bitcast_dynamic-update-slice_fusion.10
  352.3 8.0 bitcast_dynamic-update-slice_fusion.9
  362.1 11.4 %fusion.151 = f32[6,1024,1024]{1,2,0:T(8,128)} fusion(bf16[2,1024,6,64]{1,3,2,0:T(8,128)(2,1)} %get-tuple-element.434, s32[]{:T(128)S(6)} %copy.113, bf16[2,1024,6,64]{1,3,2,0:T(8,128)(2,1)S(1)} %get-tuple-element.432), kind=kOutput, calls=%fused_computation.37.clone.1 | convolution fusion | flops 805306368 | bytes 26739712 | tf_op jit(solution)/shard_map/while/body/eval_jaxpr/qhd,khd->hqk/dot_general | solution.py:42
  373.4 12.2 %bitcast_dynamic-update-slice_fusion.11 = bf16[2,1024,6,64]{1,3,2,0:T(8,128)(2,1)} fusion(bf16[2,1024,6,64]{1,3,2,0:T(8,128)(2,1)} %get-tuple-element.420, s32[]{:T(128)S(6)} %copy.113, f32[6,1024,1024]{1,2,0:T(8,128)} %fusion.151, f32[6,1024]{1,0:T(8,128)S(1)} %dynamic-slice_bitcast_fusion.2, pred[1024]{0:T(1024)(128)(4,1)S(1)} %dynamic-slice_reduce_fusion.5, ...), kind=kOutput, calls=%fused_computation.29.clone.1 | convolution fusion | flops 830472192 | bytes 27559936 | tf_op jit(solution)/shard_map/while/body/eval_jaxpr/hqk,qhd->khd/dot_general | solution.py:64
  385.7 17.2 %multiply_reduce_fusion.3 = (f32[6,1024]{1,0:T(8,128)S(1)}, f32[6,1024,1024]{1,2,0:T(8,128)}) fusion(f32[6,1024,1024]{1,2,0:T(8,128)} %fusion.151, f32[6,1024]{1,0:T(8,128)S(1)} %dynamic-slice_bitcast_fusion.2, pred[1024]{0:T(1024)(128)(4,1)S(1)} %dynamic-slice_reduce_fusion.5, bf16[2,1024,6,64]{1,3,2,0:T(8,128)(2,1)} %get-tuple-element.437, ...), kind=kOutput, calls=%fused_computation.24.clone.1 | convolution fusion | flops 836757504 | bytes 51955712 | tf_op jit(solution)/shard_map/while/body/eval_jaxpr/qhd,khd->hqk/dot_general | solution.py:67
  402.9 23.1 %multiply_convert_fusion.3 = bf16[6,1024,1024]{1,2,0:T(8,128)(2,1)} fusion(f32[6,1024,1024]{1,2,0:T(8,128)} %get-tuple-element.380, f32[6,1024,1024]{1,2,0:T(8,128)} %fusion.151, f32[6,1024]{1,0:T(8,128)S(1)} %get-tuple-element.381, f32[6,1024]{1,0:T(8,128)S(1)} %dynamic-slice_bitcast_fusion.2, pred[1024]{0:T(1024)(128)(4,1)S(1)} %dynamic-slice_reduce_fusion.5), kind=kLoop, calls=%fused_computation.23.clone.1 | loop fusion | flops 37748736 | bytes 62964736 | tf_op jit(solution)/shard_map/while/body/eval_jaxpr/convert_element_type | solution.py:69
  426.0 8.7 bitcast_dynamic-update-slice_fusion.10
  434.7 8.0 bitcast_dynamic-update-slice_fusion.9
  446.8 4.3 broadcast_multiply_fusion.1
  454.7 4.8 add_convert_fusion.3
  464.7 8.4 bitcast_convert_fusion
  473.2 9.9 %convolution_bitcast_fusion.1 = f32[768,1536]{1,0:T(8,128)} fusion(bf16[2,1024,768]{2,1,0:T(8,128)(2,1)} %all-gather.7.cloned.1.call-done, bf16[2,1024,1536]{2,1,0:T(8,128)(2,1)} %copy-done.62), kind=kOutput, calls=%fused_computation.101 | convolution fusion | flops 4831838208 | bytes 14155776 | tf_op jit(solution)/shard_map/gld,glf->df/dot_general | solution.py:172
  483.1 9.1 convolution_bitcast_fusion
  495.5 5.8 fusion.95
  506.7 81.8 %all-reduce.5 = (f32[3,384]{1,0:T(4,128)}, f32[1536]{0:T(1024)}) all-reduce(f32[3,384]{1,0:T(4,128)S(1)} %convert_reduce_fusion.1, f32[1536]{0:T(1024)S(1)} %copy-done.44), channel_id=1, replica_groups=mesh['dp'=16,'tensor'=2] {'dp'}, use_global_device_ids=true, to_apply=%region_21.22 | all-reduce | flops 2688 | bytes 21504 | tf_op jit(solution)/shard_map/psum | solution.py:243
  591.2 3.1 fusion.66
  597.1 40.4 %all-reduce.4 = (f32[768]{0:T(1024)}, f32[768]{0:T(1024)}, f32[768]{0:T(1024)}, f32[768]{0:T(1024)}, f32[768]{0:T(1024)}, /*index=5*/f32[768]{0:T(1024)}, f32[70]{0:T(128)S(1)}) all-reduce(f32[768]{0:T(1024)S(1)} %copy-done.41, f32[768]{0:T(1024)S(1)} %get-tuple-element.251, ...), channel_id=1, replica_groups=mesh['dp'=16,'tensor'=2] {'dp','tensor'}, use_global_device_ids=true, to_apply=%region_24.25 | all-reduce | flops 4678 | bytes 37424 | tf_op jit(solution)/shard_map/psum | solution.py:231
  638.0 258.6 %all-reduce.9.cloned.1.call-done = (f32[3,768,384]{1,2,0:T(8,128)}, f32[384,768]{1,0:T(8,128)}, f32[768,1536]{1,0:T(8,128)}, f32[1536,768]{1,0:T(8,128)}) async-done(((f32[3,768,384]{1,2,0:T(8,128)}, f32[384,768]{1,0:T(8,128)}, f32[768,1536]{1,0:T(8,128)}, f32[1536,768]{1,0:T(8,128)}), (f32[3,768,384]{1,2,0:T(8,128)}, f32[384,768]{1,0:T(8,128)}, f32[768,1536]{1,0:T(8,128)}, ...) | async-done | bytes 14155792 | tf_op jit(solution)/shard_map/psum | solution.py:243
  896.6 5.2 copy.82
  902.9 5.5 copy.126
  (229 shorter events, 66.4 us)
Async XLA Ops:
  7.2 146.2 %copy-start = (bf16[768,1536]{1,0:T(8,128)(2,1)S(1)}, bf16[768,1536]{1,0:T(8,128)(2,1)}, u32[]{:S(2)}) copy-start(bf16[768,1536]{1,0:T(8,128)(2,1)} %param.27) | copy-start | bytes 7077892
  7.2 23.4 %all-gather.5.cloned.1.call-start = ((), (), s32[]{:S(2)}) async-start(), calls=%async_computation.4 | async-start | bytes 4718592 | tf_op jit(solution)/shard_map/all_gather | solution.py:116
  7.2 6.6 copy-start.2
  10.6 5.1 copy-start.47
  15.6 118.5 %reduce-scatter.5.cloned.1.call-start = ((), (), s32[]{:S(2)}) async-start(), calls=%async_computation.5 | async-start | bytes 4718592 | tf_op jit(solution)/shard_map/reduce_scatter | solution.py:136
  16.8 24.2 %copy-start.26 = (f32[1024,64]{0,1:T(8,128)}, f32[1024,64]{0,1:T(8,128)S(1)}, u32[]{:S(2)}) copy-start(f32[1024,64]{0,1:T(8,128)S(1)} %get-tuple-element.259) | copy-start | bytes 786436
  16.8 24.2 %copy-start.28 = (f32[1024,64]{0,1:T(8,128)}, f32[1024,64]{0,1:T(8,128)S(1)}, u32[]{:S(2)}) copy-start(f32[1024,64]{0,1:T(8,128)S(1)} %get-tuple-element.260) | copy-start | bytes 786436
  44.0 72.6 %copy-start.58 = (bf16[384,768]{1,0:T(8,128)(2,1)S(1)}, bf16[384,768]{1,0:T(8,128)(2,1)}, u32[]{:S(2)}) copy-start(bf16[384,768]{1,0:T(8,128)(2,1)} %param.25) | copy-start | bytes 1769476
  56.2 11.9 %copy-start.11 = (bf16[2,1024,6,64]{1,3,2,0:T(8,128)(2,1)S(1)}, bf16[2,1024,6,64]{1,3,2,0:T(8,128)(2,1)}, u32[]{:S(2)}) copy-start(bf16[2,1024,6,64]{1,3,2,0:T(8,128)(2,1)} %get-tuple-element.401) | copy-start | bytes 4718596 | tf_op jit(solution)/shard_map/while
  56.2 11.9 %copy-start.59 = (bf16[2,1024,6,64]{1,3,2,0:T(8,128)(2,1)S(1)}, bf16[2,1024,6,64]{1,3,2,0:T(8,128)(2,1)}, u32[]{:S(2)}) copy-start(bf16[2,1024,6,64]{1,3,2,0:T(8,128)(2,1)} %get-tuple-element.391) | copy-start | bytes 4718596 | tf_op jit(solution)/shard_map/while
  92.3 11.9 %copy-start.11 = (bf16[2,1024,6,64]{1,3,2,0:T(8,128)(2,1)S(1)}, bf16[2,1024,6,64]{1,3,2,0:T(8,128)(2,1)}, u32[]{:S(2)}) copy-start(bf16[2,1024,6,64]{1,3,2,0:T(8,128)(2,1)} %get-tuple-element.401) | copy-start | bytes 4718596 | tf_op jit(solution)/shard_map/while
  92.4 11.9 %copy-start.59 = (bf16[2,1024,6,64]{1,3,2,0:T(8,128)(2,1)S(1)}, bf16[2,1024,6,64]{1,3,2,0:T(8,128)(2,1)}, u32[]{:S(2)}) copy-start(bf16[2,1024,6,64]{1,3,2,0:T(8,128)(2,1)} %get-tuple-element.391) | copy-start | bytes 4718596 | tf_op jit(solution)/shard_map/while
  121.6 31.8 %all-gather.7.cloned.1.call-start = ((), (), s32[]{:S(2)}) async-start(), calls=%async_computation.6 | async-start | bytes 4718592 | tf_op jit(solution)/shard_map/all_gather | solution.py:148
  139.8 60.0 %all-gather.9.cloned.1.call-start = ((), (), s32[]{:S(2)}) async-start(), calls=%async_computation.8 | async-start | bytes 4718592 | tf_op jit(solution)/shard_map/all_gather | solution.py:165
  140.4 98.6 %reduce-scatter.9.cloned.1.call-start = ((), (), s32[]{:S(2)}) async-start(), calls=%async_computation.9 | async-start | bytes 4718592 | tf_op jit(solution)/shard_map/reduce_scatter | solution.py:174
  226.4 27.7 %reduce-scatter.7.cloned.1.call-start = ((), (), s32[]{:S(2)}) async-start(), calls=%async_computation.7 | async-start | bytes 4718592 | tf_op jit(solution)/shard_map/reduce_scatter | solution.py:154
  237.3 37.7 %all-gather.11.cloned.1.call-start = ((), (), s32[]{:S(2)}) async-start(), calls=%async_computation.10 | async-start | bytes 4718592 | tf_op jit(solution)/shard_map/all_gather | solution.py:186
  261.5 327.0 %reduce-scatter.11.cloned.1.call-start = ((), (), s32[]{:S(2)}) async-start(), calls=%async_computation.11 | async-start | bytes 4718592 | tf_op jit(solution)/shard_map/reduce_scatter | solution.py:206
  261.5 17.9 %copy-start.6 = (bf16[2,1024,6,64]{1,3,2,0:T(8,128)(2,1)S(1)}, bf16[2,1024,6,64]{1,3,2,0:T(8,128)(2,1)}, u32[]{:S(2)}) copy-start(bf16[2,1024,6,64]{1,3,2,0:T(8,128)(2,1)} %get-tuple-element.470) | copy-start | bytes 4718596
  279.7 11.4 %copy-start.22 = (bf16[2,1024,6,64]{1,3,2,0:T(8,128)(2,1)S(1)}, bf16[2,1024,6,64]{1,3,2,0:T(8,128)(2,1)}, u32[]{:S(2)}) copy-start(bf16[2,1024,6,64]{1,3,2,0:T(8,128)(2,1)} %get-tuple-element.436) | copy-start | bytes 4718596 | tf_op jit(solution)/shard_map/while
  320.5 23.1 %copy-start.7 = (bf16[2,1024,6,64]{1,3,2,0:T(8,128)(2,1)S(1)}, bf16[2,1024,6,64]{1,3,2,0:T(8,128)(2,1)}, u32[]{:S(2)}) copy-start(bf16[2,1024,6,64]{1,3,2,0:T(8,128)(2,1)} %get-tuple-element.434) | copy-start | bytes 4718596 | tf_op jit(solution)/shard_map/while
  320.5 23.1 %copy-start.16 = (f32[2,1024,6,64]{1,3,2,0:T(8,128)S(1)}, f32[2,1024,6,64]{1,3,2,0:T(8,128)}, u32[]{:S(2)}) copy-start(f32[2,1024,6,64]{1,3,2,0:T(8,128)} %get-tuple-element.419) | copy-start | bytes 9437188 | tf_op jit(solution)/shard_map/while
  343.6 8.7 copy-start.19
  352.3 8.0 copy-start.17
  362.1 11.4 %copy-start.22 = (bf16[2,1024,6,64]{1,3,2,0:T(8,128)(2,1)S(1)}, bf16[2,1024,6,64]{1,3,2,0:T(8,128)(2,1)}, u32[]{:S(2)}) copy-start(bf16[2,1024,6,64]{1,3,2,0:T(8,128)(2,1)} %get-tuple-element.436) | copy-start | bytes 4718596 | tf_op jit(solution)/shard_map/while
  402.9 23.1 %copy-start.7 = (bf16[2,1024,6,64]{1,3,2,0:T(8,128)(2,1)S(1)}, bf16[2,1024,6,64]{1,3,2,0:T(8,128)(2,1)}, u32[]{:S(2)}) copy-start(bf16[2,1024,6,64]{1,3,2,0:T(8,128)(2,1)} %get-tuple-element.434) | copy-start | bytes 4718596 | tf_op jit(solution)/shard_map/while
  402.9 23.1 %copy-start.16 = (f32[2,1024,6,64]{1,3,2,0:T(8,128)S(1)}, f32[2,1024,6,64]{1,3,2,0:T(8,128)}, u32[]{:S(2)}) copy-start(f32[2,1024,6,64]{1,3,2,0:T(8,128)} %get-tuple-element.419) | copy-start | bytes 9437188 | tf_op jit(solution)/shard_map/while
  426.0 8.7 copy-start.19
  434.7 8.0 copy-start.17
  446.7 47.9 %copy-start.23 = (bf16[1,2,1024,384]{3,2,0,1:T(8,128)(2,1)}, bf16[1,2,1024,384]{3,2,0,1:T(8,128)(2,1)S(1)}, u32[]{:S(2)}) copy-start(bf16[1,2,1024,384]{3,2,0,1:T(8,128)(2,1)S(1)} %copy.78) | copy-start | bytes 4718596
  473.1 423.5 %all-reduce.9.cloned.1.call-start = ((), (), s32[]{:S(2)}) async-start(), calls=%async_computation.12 | async-start | bytes 28311552 | tf_op jit(solution)/shard_map/psum | solution.py:243
  473.2 9.9 %copy-start.55 = (bf16[2,1024,768]{2,1,0:T(8,128)(2,1)S(1)}, bf16[2,1024,768]{2,1,0:T(8,128)(2,1)}, u32[]{:S(2)}) copy-start(bf16[2,1024,768]{2,1,0:T(8,128)(2,1)} %all-gather.9.cloned.1.call-done) | copy-start | bytes 9437188
  483.1 9.1 copy-start.56
  483.1 9.1 copy-start.61
  501.3 5.3 copy-start.44
  501.3 87.2 %copy-start.5 = (bf16[1,1024,768]{2,1,0:T(8,128)(2,1)S(1)}, bf16[1,1024,768]{2,1,0:T(8,128)(2,1)}, u32[]{:S(2)}) copy-start(bf16[1,1024,768]{2,1,0:T(8,128)(2,1)} %param.20) | copy-start | bytes 4718596
  501.3 87.2 %copy-start.32 = (f32[1024]{0:T(1024)S(1)}, f32[1024]{0:T(1024)}, u32[]{:S(2)}) copy-start(f32[1024]{0:T(1024)} %copy-done.31) | copy-start | bytes 12292
  501.4 87.2 %copy-start.34 = (f32[768]{0:T(1024)S(1)}, f32[768]{0:T(1024)}, u32[]{:S(2)}) copy-start(f32[768]{0:T(1024)} %copy-done.33) | copy-start | bytes 9220
  504.0 87.2 %copy-start.40 = (f32[1024]{0:T(1024)S(1)}, f32[1024]{0:T(1024)}, u32[]{:S(2)}) copy-start(f32[1024]{0:T(1024)} %copy-done.39) | copy-start | bytes 12292
  504.0 87.3 %copy-start.36 = (f32[1024]{0:T(1024)S(1)}, f32[1024]{0:T(1024)}, u32[]{:S(2)}) copy-start(f32[1024]{0:T(1024)} %copy-done.35) | copy-start | bytes 12292
  588.5 5.9 copy-start.38
  588.5 5.9 copy-start.10
  588.5 5.9 copy-start.12
  588.5 5.9 copy-start.14
  896.6 5.3 copy-start.30
  901.9 6.5 slice-start
  902.9 5.5 slice-start.1
  902.9 7.7 copy-start.1
  (35 other events, 91.8 us)
Sparse Core Ops, SparseCore 0:
  15.7 14.8 all-gather.4
  121.7 12.3 reduce-scatter.4
  140.0 13.3 all-gather.6
  154.8 13.2 all-gather.8
  226.5 12.3 reduce-scatter.8
  241.7 12.4 reduce-scatter.6
  261.6 13.3 all-gather.10
  473.3 12.3 reduce-scatter.10
  501.4 395.1 all-reduce.8
where the time goes:
time: 925 us; the launch traced here: 917 us
  waiting for transfers between devices  324 us (35%)
  matrix products  257 us (28%)
  other arithmetic  154 us (17%)
  blocking collectives  122 us (13%)
  local copies, waits for them, and re-layouts  44.4 us (5%)
  between operations  14.8 us (2%)
    psum x1, waiting for transfers between devices, per_device(): lax.psum((grad_w_qkv, grad_b_qkv, grad_w_out, grad_w_up, grad_b_up, grad_...  259 us
    psum x1, blocking collectives, per_device(): lax.psum((grad_w_qkv, grad_b_qkv, grad_w_out, grad_w_up, grad_b_up, grad_...  81.8 us
    dot_general x4, matrix products, masked_scores(): jnp.einsum('qhd,khd->hqk', queries, keys_rot, preferred_element_type=jnp....  46.5 us
    convert_element_type x2, other arithmetic, attend_backward(): grad_scores = (prob_full * (grad_probs - row_delta)).astype(jnp.bfloat16)  46.2 us
    psum x1, blocking collectives, per_device(): lax.psum((grad_first_gain, grad_first_bias, grad_second_gain, grad_second...  40.4 us
    dot_general x2, matrix products, attend_backward(): jnp.einsum('qhd,khd->hqk', grad_mixed, values, preferred_element_type=jnp...  34.5 us
    convert_element_type x1, other arithmetic, per_device(): act_low = activation.astype(jnp.bfloat16)  30.9 us
    unnamed x116, local copies, waits for them, and re-layouts  28.5 us
  transfers between devices with their start and end apart: 9, of which 7 were waited for; matrix products, arithmetic and copies ran while one was open for 11% of the time, Pallas kernels for 0%

commit v1 on v0

v1 whole, which is shorter than its diff:
```python
import functools

import jax
import jax.numpy as jnp
import numpy as np
from jax import lax
from jax.experimental import pallas as pl
from jax.experimental.pallas import tpu as pltpu
from jax.sharding import PartitionSpec as P

HEAD_DIM = 64
CLASSES = 70
EPSILON = 1e-05
PAIR = 2 * HEAD_DIM
BF = jnp.bfloat16
F32 = jnp.float32
NN = (((1,), (0,)), ((), ()))
NT = (((1,), (1,)), ((), ()))
VMEM_LIMIT = 60 * 1024 * 1024

ERF_P = 0.39
ERF_C = (
    0.2353350342991649,
    0.09132489362337098,
    0.6497226730753285,
    -0.6356086817390623,
    0.886796488962974,
    -0.22757041290383279,
)


def dot(a, b, dims):
    return lax.dot_general(a, b, dims, preferred_element_type=F32)


def call(body, grid, in_specs, out_specs, out_shape, flops, nbytes, scratch=(), name=None):
    return pl.pallas_call(
        body,
        grid=grid,
        in_specs=in_specs,
        out_specs=out_specs,
        out_shape=out_shape,
        scratch_shapes=list(scratch),
        compiler_params=pltpu.CompilerParams(vmem_limit_bytes=VMEM_LIMIT),
        cost_estimate=pl.CostEstimate(
            flops=int(flops), bytes_accessed=int(nbytes), transcendentals=0
        ),
        name=name,
    )


def rope_tables(length):
    half = HEAD_DIM // 2
    freq = np.float32(10000.0) ** (-2.0 * np.arange(half).astype(np.float32) / np.float32(HEAD_DIM))
    angles = np.arange(length).astype(np.float32)[:, None] * freq.astype(np.float32)[None, :]
    cosine = np.cos(angles)
    sine = np.sin(angles)
    cosine = np.concatenate([cosine, cosine, cosine, cosine], axis=1)
    sine = np.concatenate([-sine, sine, -sine, sine], axis=1)
    return cosine.astype(np.float32), sine.astype(np.float32)


def turn(v):
    lane = lax.broadcasted_iota(jnp.int32, v.shape, 1)
    first = lax.rem(lane, HEAD_DIM) < HEAD_DIM // 2
    half = HEAD_DIM // 2
    return jnp.where(first, pltpu.roll(v, PAIR - half, 1), pltpu.roll(v, half, 1))


def ln_forward(x):
    centred = x - jnp.mean(x, axis=-1, keepdims=True)
    scale = lax.rsqrt(jnp.mean(centred * centred, axis=-1, keepdims=True) + EPSILON)
    return centred * scale, scale


def ln_backward(xhat, scale, grad, gain):
    h = grad * gain
    mean_h = jnp.mean(h, axis=-1, keepdims=True)
    mean_hx = jnp.mean(h * xhat, axis=-1, keepdims=True)
    return scale * (h - mean_h - xhat * mean_hx)


def full(shape):
    zeros = (0,) * len(shape)
    return pl.BlockSpec(shape, lambda *_: zeros)


def project_body(normalize, *refs):
    if normalize:
        x_ref, g_ref, b_ref, w_ref, bias_ref, cos_ref, sin_ref, n_ref, q_ref, k_ref, v_ref = refs
        xhat, _ = ln_forward(x_ref[...].astype(F32))
        normed = (xhat * g_ref[...] + b_ref[...]).astype(BF)
        n_ref[...] = normed
    else:
        n_ref, w_ref, bias_ref, cos_ref, sin_ref, q_ref, k_ref, v_ref = refs
        normed = n_ref[...]
    cosine, sine = cos_ref[...], sin_ref[...]
    width = w_ref.shape[2]
    for c, out in ((0, q_ref), (1, k_ref), (2, v_ref)):
        y = dot(normed, w_ref[c], NN) + bias_ref[c : c + 1, :]
        if c == 2:
            out[...] = y.astype(BF)
            continue
        for p in range(width // PAIR):
            piece = y[:, p * PAIR : (p + 1) * PAIR]
            piece = piece * cosine + turn(piece) * sine
            if c == 0:
                piece = piece * (HEAD_DIM**-0.5)
            out[:, p * PAIR : (p + 1) * PAIR] = piece.astype(BF)


def project(x, gain, bias, w, b, cosine, sine, normalize):
    length, width = x.shape
    half = w.shape[2]
    rows = 256
    row = lambda n: pl.BlockSpec((rows, n), lambda i: (i, 0))
    head = [x, gain, bias] if normalize else [x]
    head_specs = [row(width)] + ([full((1, width))] * 2 if normalize else [])
    outs = [jax.ShapeDtypeStruct((length, half), BF)] * 3
    out_specs = [row(half)] * 3
    if normalize:
        outs = [jax.ShapeDtypeStruct((length, width), BF)] + outs
        out_specs = [row(width)] + out_specs
    return call(
        functools.partial(project_body, normalize),
        (length // rows,),
        head_specs + [full(w.shape), full(b.shape), row(PAIR), row(PAIR)],
        out_specs,
        outs,
        2 * length * width * half * 3,
        2 * (length * width * 2 + 3 * width * half + 3 * length * half),
        name="project",
    )(*head, w, b, cosine, sine)


def attend_body(len_ref, q_ref, k_ref, v_ref, e_ref, ot_ref, o_ref, linv_ref):
    length = q_ref.shape[0]
    step = 256
    valid = lax.broadcasted_iota(jnp.int32, (length, PAIR), 0) < len_ref[0]
    lane = lax.broadcasted_iota(jnp.int32, (length, PAIR), 1)
    q, k = q_ref[...], k_ref[...]
    v_t = jnp.transpose(v_ref[...])
    ones = jnp.ones((16, length), BF)
    mask = jnp.where(valid, 0.0, -1.0e9).astype(BF)
    work = []
    for h in range(2):
        other = HEAD_DIM * (1 - h)
        own = (lane >= HEAD_DIM * h) & (lane < HEAD_DIM * (h + 1))
        q_h = jnp.where(own, q, jnp.where(lane == other, 1.0, 0.0).astype(BF))
        k_h = jnp.where(lane == other, mask, k)
        v_h = jnp.concatenate([v_t[HEAD_DIM * h : HEAD_DIM * (h + 1)], ones], axis=0)
        for c in range(length // step):
            work.append((h, c, q_h, k_h, v_h))

    def scores(item):
        h, c, q_h, k_h, v_h = item
        return dot(k_h, q_h[c * step : (c + 1) * step], NT)

    ahead = scores(work[0])
    for i, item in enumerate(work):
        h, c, q_h, k_h, v_h = item
        now = ahead
        if i + 1 < len(work):
            ahead = scores(work[i + 1])
        where = slice(c * step, (c + 1) * step)
        top = jnp.max(now, axis=0, keepdims=True)
        e = jnp.exp(now - top).astype(BF)
        e_ref[h, :, where] = e
        o = dot(v_h, e, NN)
        linv = 1.0 / o[HEAD_DIM : HEAD_DIM + 1]
        linv_ref[0, h : h + 1, where] = linv
        ot_ref[HEAD_DIM * h : HEAD_DIM * (h + 1), where] = (o[:HEAD_DIM] * linv).astype(BF)
    o_ref[...] = jnp.transpose(ot_ref[...])


def attend(own_length, q, k, v):
    length, half = q.shape
    pairs = half // PAIR
    col = pl.BlockSpec((length, PAIR), lambda p: (0, p))
    return call(
        attend_body,
        (pairs,),
        [pl.BlockSpec(memory_space=pltpu.SMEM), col, col, col],
        [
            pl.BlockSpec((2, length, length), lambda p: (p, 0, 0)),
            pl.BlockSpec((PAIR, length), lambda p: (p, 0)),
            col,
            pl.BlockSpec((1, 8, length), lambda p: (p, 0, 0)),
        ],
        [
            jax.ShapeDtypeStruct((2 * pairs, length, length), BF),
            jax.ShapeDtypeStruct((half, length), BF),
            jax.ShapeDtypeStruct((length, half), BF),
            jax.ShapeDtypeStruct((pairs, 8, length), F32),
        ],
        2 * 4 * length * length * PAIR * pairs,
        4 * pairs * length * length,
        name="attend",
    )(own_length, q, k, v)


def attend_grad_body(
    e_ref, linv_ref, q_ref, k_ref, v_ref, ot_ref, dot_ref, cos_ref, sin_ref, dq_ref, dk_ref, dv_ref
):
    length = q_ref.shape[0]
    step = 256
    lane = lax.broadcasted_iota(jnp.int32, (length, PAIR), 1)
    q, v = q_ref[...], v_ref[...]
    k_t = jnp.transpose(k_ref[...])
    zeros = jnp.zeros((HEAD_DIM, length), BF)
    work = []
    for h in range(2):
        rows = slice(HEAD_DIM * h, HEAD_DIM * (h + 1))
        own = (lane >= HEAD_DIM * h) & (lane < HEAD_DIM * (h + 1))
        q_h = jnp.where(own, q, jnp.zeros_like(q))
        d_o = dot_ref[rows, :].astype(F32) * linv_ref[0, h : h + 1, :]
        delta = jnp.sum(d_o * ot_ref[rows, :].astype(F32), axis=0, keepdims=True)
        d_low = d_o.astype(BF)
        d_pad = jnp.concatenate([d_low, zeros] if h == 0 else [zeros, d_low], axis=0)
        for c in range(length // step):
            work.append((h, c, q_h, d_pad, delta, k_t[rows]))

    def grad_probs(item):
        h, c, q_h, d_pad, delta, k_h = item
        return dot(v, d_pad[:, c * step : (c + 1) * step], NN)

    d_v = jnp.zeros((length, PAIR), F32)
    d_k = jnp.zeros((length, PAIR), F32)
    d_q = [[], []]
    ahead = grad_probs(work[0])
    for i, item in enumerate(work):
        h, c, q_h, d_pad, delta, k_h = item
        now = ahead
        if i + 1 < len(work):
            ahead = grad_probs(work[i + 1])
        where = slice(c * step, (c + 1) * step)
        e = e_ref[h, :, where]
        d_s = (e.astype(F32) * (now - delta[:, where])).astype(BF)
        d_v = d_v + dot(e, d_pad[:, where], NT)
        d_k = d_k + dot(d_s, q_h[where], NN)
        d_q[h].append(dot(k_h, d_s, NN))
    cosine, sine = cos_ref[...], sin_ref[...]
    dv_ref[...] = d_v.astype(BF)
    dk_ref[...] = (d_k * cosine - turn(d_k) * sine).astype(BF)
    both = [jnp.concatenate(parts, axis=1) for parts in d_q]
    both = jnp.transpose(jnp.concatenate(both, axis=0)) * (HEAD_DIM**-0.5)
    dq_ref[...] = (both * cosine - turn(both) * sine).astype(BF)


def attend_grad(e, linv, q, k, v, o_t, do_t, cosine, sine):
    length, half = q.shape
    pairs = half // PAIR
    col = pl.BlockSpec((length, PAIR), lambda p: (0, p))
    row = pl.BlockSpec((PAIR, length), lambda p: (p, 0))
    return call(
        attend_grad_body,
        (pairs,),
        [
            pl.BlockSpec((2, length, length), lambda p: (p, 0, 0)),
            pl.BlockSpec((1, 8, length), lambda p: (p, 0, 0)),
            col,
            col,
            col,
            row,
            row,
            full((length, PAIR)),
            full((length, PAIR)),
        ],
        [col] * 3,
        [jax.ShapeDtypeStruct((length, half), BF)] * 3,
        2 * 8 * length * length * PAIR * pairs,
        4 * pairs * length * length,
        name="attend_grad",
    )(e, linv, q, k, v, o_t, do_t, cosine, sine)


def out_body(o1_ref, o2_ref, w1_ref, w2_ref, x_ref, b_ref, g_ref, s_ref, res_ref, n_ref):
    res = dot(o1_ref[...], w1_ref[...], NN) + dot(o2_ref[...], w2_ref[...], NN)
    res = x_ref[...].astype(F32) + (res + b_ref[...])
    res_ref[...] = res
    xhat, _ = ln_forward(res)
    n_ref[...] = (xhat * g_ref[...] + s_ref[...]).astype(BF)


def out_project(o1, o2, w1, w2, x, b_out, gain, bias):
    length, width = x.shape
    half = w1.shape[0]
    rows = 256
    row = lambda n: pl.BlockSpec((rows, n), lambda i: (i, 0))
    return call(
        out_body,
        (length // rows,),
        [row(half), row(half), full(w1.shape), full(w2.shape), row(width)] + [full((1, width))] * 3,
        [row(width)] * 2,
        [jax.ShapeDtypeStruct((length, width), F32), jax.ShapeDtypeStruct((length, width), BF)],
        2 * length * width * half * 2,
        length * width * 10,
        name="out_project",
    )(o1, o2, w1, w2, x, b_out, gain, bias)


def gelu_parts(u):
    z = jnp.abs(u) * (0.5**0.5)
    t = 1.0 / (1.0 + ERF_P * z)
    poly = jnp.full_like(t, ERF_C[-1])
    for coef in ERF_C[-2::-1]:
        poly = poly * t + coef
    e = jnp.exp(u * u * -0.5)
    tail = 0.5 * (poly * t) * e
    cdf = jnp.where(u >= 0, 1.0 - tail, tail)
    return u * cdf, cdf + u * (e * 0.3989422804014327)


def mlp_body(last, *refs):
    if last:
        (n_ref, ct_ref, wu_ref, bu_ref, wd_ref, ff_in, dn_in, res_ref, bd_ref, g_ref) = refs[:10]
        (dwu_ref, dwd_ref, dbu_ref, y_ref, gres_ref, ga_ref, vec_ref, ff_ref, dn_ref, nt_ref) = refs[10:]
    else:
        n_ref, ct_ref, wu_ref, bu_ref, wd_ref = refs[:5]
        dwu_ref, dwd_ref, dbu_ref, ff_ref, dn_ref, nt_ref = refs[5:]
    j = pl.program_id(0)

    @pl.when(j == 0)
    def _():
        nt_ref[...] = jnp.transpose(n_ref[...])
        if last:
            ff_ref[...] = ff_in[...]
            dn_ref[...] = dn_in[...]
        else:
            ff_ref[...] = jnp.zeros_like(ff_ref)
            dn_ref[...] = jnp.zeros_like(dn_ref)

    n, ct, wu, wd = n_ref[...], ct_ref[...], wu_ref[...], wd_ref[...]
    up = dot(n, wu, NN) + bu_ref[...]
    d_act = dot(ct, wd, NT)
    act, slope = gelu_parts(up)
    act = act.astype(BF)
    d_up = (d_act * slope).astype(BF)
    ff_ref[...] += dot(act, wd, NN)
    dwd_ref[...] = dot(jnp.transpose(act), ct, NN).astype(BF)
    dwu_ref[...] = dot(nt_ref[...], d_up, NN).astype(BF)
    dn_ref[...] += dot(d_up, wu, NT)
    dbu_ref[...] = jnp.sum(d_up.astype(F32), axis=0, keepdims=True)

    if last:

        @pl.when(j == pl.num_programs(0) - 1)
        def _():
            length = n_ref.shape[0]
            step = 128
            vec_ref[...] = jnp.zeros_like(vec_ref)

            def tail(i, carry):
                at = pl.ds(pl.multiple_of(i * step, step), step)
                res = res_ref[at, :]
                y_ref[at, :] = (res + (ff_ref[at, :] + bd_ref[...])).astype(BF)
                xhat, scale = ln_forward(res)
                d_n = dn_ref[at, :]
                c = ct_ref[at, :].astype(F32)
                g_res = c + ln_backward(xhat, scale, d_n, g_ref[...])
                gres_ref[at, :] = g_res
                low = g_res.astype(BF)
                ga_ref[at, :] = low
                vec_ref[0:1, :] += jnp.sum(d_n * xhat, axis=0, keepdims=True)
                vec_ref[1:2, :] += jnp.sum(d_n, axis=0, keepdims=True)
                vec_ref[2:3, :] += jnp.sum(low.astype(F32), axis=0, keepdims=True)
                vec_ref[3:4, :] += jnp.sum(c, axis=0, keepdims=True)
                return carry

            lax.fori_loop(0, length // step, tail, 0)


def mlp(n, ct, wu, bu, wd, rest=None):
    length, width = n.shape
    half = wu.shape[1]
    block = 512
    last = rest is not None
    whole = full((length, width))
    grad_specs = [
        pl.BlockSpec((width, block), lambda j: (0, j)),
        pl.BlockSpec((block, width), lambda j: (j, 0)),
        pl.BlockSpec((1, block), lambda j: (0, j)),
    ]
    in_specs = [
        whole,
        whole,
        grad_specs[0],
        grad_specs[2],
        grad_specs[1],
    ]
    args = [n, ct, wu, bu, wd]
    outs = [
        jax.ShapeDtypeStruct((width, half), BF),
        jax.ShapeDtypeStruct((half, width), BF),
        jax.ShapeDtypeStruct((1, half), F32),
    ]
    out_specs = list(grad_specs)
    big = jax.ShapeDtypeStruct((length, width), F32)
    low = jax.ShapeDtypeStruct((length, width), BF)
    scratch = [pltpu.VMEM((width, length), BF)]
    if last:
        args += list(rest)
        in_specs += [whole, whole, whole, full((1, width)), full((1, width))]
        outs += [low, big, low, jax.ShapeDtypeStruct((8, width), F32)]
        out_specs += [whole, whole, whole, full((8, width))]
        scratch = [pltpu.VMEM((length, width), F32)] * 2 + scratch
    else:
        outs += [big, big]
        out_specs += [whole, whole]
    return call(
        functools.partial(mlp_body, last),
        (half // block,),
        in_specs,
        out_specs,
        outs,
        2 * length * width * half * 6,
        length * width * 20 + 8 * width * half,
        scratch,
        name="mlp_last" if last else "mlp_first",
    )(*args)


def mixed_grad_body(w_ref, ot_ref, ga_ref, dm_ref, dw_ref):
    ga = ga_ref[...]
    dm_ref[...] = dot(w_ref[...], ga, NT).astype(BF)
    dw_ref[...] = dot(ot_ref[...], ga, NN).astype(BF)


def mixed_grad(w, o_t, ga):
    half, width = w.shape
    length = ga.shape[0]
    rows = PAIR
    row = lambda n: pl.BlockSpec((rows, n), lambda i: (i, 0))
    return call(
        mixed_grad_body,
        (half // rows,),
        [row(width), row(length), full(ga.shape)],
        [row(length), row(width)],
        [jax.ShapeDtypeStruct((half, length), BF), jax.ShapeDtypeStruct((half, width), BF)],
        4 * length * width * half,
        2 * (2 * half * length + length * width + 2 * half * width),
        name="mixed_grad",
    )(w, o_t, ga)


def weight_grad_body(n_ref, dq_ref, dk_ref, dv_ref, dw_ref, db_ref, nt_ref):
    nt_ref[...] = jnp.transpose(n_ref[...])
    for c, ref in enumerate((dq_ref, dk_ref, dv_ref)):
        d = ref[...]
        dw_ref[c] = dot(nt_ref[...], d, NN).astype(BF)
        db_ref[c : c + 1, :] = jnp.sum(d.astype(F32), axis=0, keepdims=True)


def weight_grad(n, grads):
    length, width = n.shape
    half = grads[0].shape[1]
    return call(
        weight_grad_body,
        (1,),
        [full(n.shape)] + [full((length, half))] * 3,
        [full((3, width, half)), full((3, half))],
        [jax.ShapeDtypeStruct((3, width, half), BF), jax.ShapeDtypeStruct((3, half), F32)],
        2 * length * width * half * 3,
        2 * (length * width + 3 * length * half + 3 * width * half),
        [pltpu.VMEM((width, length), BF)],
        name="weight_grad",
    )(n, *grads)


def input_grad_body(*refs):
    grads, (w1_ref, w2_ref, x_ref, gres_ref, g_ref), (out_ref, vec_ref) = (
        refs[:6],
        refs[6:11],
        refs[11:],
    )
    d_n = None
    for i, ref in enumerate(grads):
        term = dot(ref[...], (w1_ref if i < 3 else w2_ref)[i % 3], NT)
        d_n = term if d_n is None else d_n + term
    xhat, scale = ln_forward(x_ref[...].astype(F32))
    out_ref[...] = (gres_ref[...] + ln_backward(xhat, scale, d_n, g_ref[...])).astype(BF)

    @pl.when(pl.program_id(0) == 0)
    def _():
        vec_ref[...] = jnp.zeros_like(vec_ref)

    vec_ref[0:1, :] += jnp.sum(d_n * xhat, axis=0, keepdims=True)
    vec_ref[1:2, :] += jnp.sum(d_n, axis=0, keepdims=True)


def input_gradient(grads1, grads2, w1, w2, x, g_res, gain):
    length, width = x.shape
    half = grads1[0].shape[1]
    rows = 256
    row = lambda n: pl.BlockSpec((rows, n), lambda i: (i, 0))
    return call(
        input_grad_body,
        (length // rows,),
        [row(half)] * 6 + [full(w1.shape), full(w2.shape), row(width), row(width), full((1, width))],
        [row(width), full((8, width))],
        [jax.ShapeDtypeStruct((length, width), BF), jax.ShapeDtypeStruct((8, width), F32)],
        2 * length * width * half * 6,
        length * width * 20,
        name="input_grad",
    )(*grads1, *grads2, w1, w2, x, g_res, gain)


def per_device(
    layer_input,
    lengths,
    predicted,
    w_qkv,
    b_qkv,
    w_out,
    b_out,
    w_up,
    b_up,
    w_down,
    b_down,
    first_gain,
    first_bias,
    second_gain,
    second_bias,
    cotangent,
):
    own_seqs, length, width = layer_input.shape
    assert own_seqs == 1 and lax.axis_size("tensor") == 2
    swap = lambda v: lax.ppermute(v, "tensor", [(0, 1), (1, 0)])
    own_length = lax.dynamic_slice_in_dim(lengths, lax.axis_index("tensor"), 1, 0)
    x, ct = layer_input[0], cotangent[0]
    row = lambda v: v.astype(F32)[None, :]
    cosine, sine = (jnp.asarray(t) for t in rope_tables(length))

    w_qkv2 = swap(w_qkv)
    b_qkv2, w_out2, w_up2, b_up2, w_down2 = (swap(v) for v in (b_qkv, w_out, w_up, b_up, w_down))

    normed, *qkv1 = project(
        x, row(first_gain), row(first_bias), w_qkv, b_qkv.astype(F32), cosine, sine, True
    )
    e1, ot1, o1, linv1 = attend(own_length, *qkv1)
    qkv2 = project(normed, None, None, w_qkv2, b_qkv2.astype(F32), cosine, sine, False)
    e2, ot2, o2, linv2 = attend(own_length, *qkv2)
    residual, normed_two = out_project(
        o1, o2, w_out, w_out2, x, row(b_out), row(second_gain), row(second_bias)
    )
    dwu2, dwd2, dbu2, ff, dn = mlp(normed_two, ct, w_up2, row(b_up2), w_down2)
    dwu1, dwd1, dbu1, y, g_res, ga, vec2 = mlp(
        normed_two, ct, w_up, row(b_up), w_down, (ff, dn, residual, row(b_down), row(second_gain))
    )
    dmt2, dwo2 = mixed_grad(w_out2, ot2, ga)
    dmt1, dwo1 = mixed_grad(w_out, ot1, ga)
    grads2 = attend_grad(e2, linv2, *qkv2, ot2, dmt2, cosine, sine)
    dwq2, dbq2 = weight_grad(normed, grads2)
    grads1 = attend_grad(e1, linv1, *qkv1, ot1, dmt1, cosine, sine)
    dwq1, dbq1 = weight_grad(normed, grads1)
    input_grad, vec1 = input_gradient(grads1, grads2, w_qkv, w_qkv2, x, g_res, row(first_gain))

    def total(own, other):
        return lax.psum(own + swap(other), "dp").astype(F32)

    grad_w_up = total(dwu1, dwu2)
    grad_w_down = total(dwd1, dwd2)
    grad_w_out = total(dwo1, dwo2)
    grad_w_qkv = total(dwq1, dwq2)
    grad_b_qkv = total(dbq1, dbq2)
    grad_b_up = total(dbu1, dbu2)[0]

    classes = jnp.arange(CLASSES)
    valid = jnp.arange(length)[None, :] < own_length
    hits = (predicted == classes[:, None]) & valid
    counts = jnp.sum(hits.astype(F32), axis=1)
    vec, counts = lax.psum((jnp.concatenate([vec1[:2], vec2[:4]]), counts), ("dp", "tensor"))
    total_tokens = length * 2 * lax.axis_size("dp")
    return (
        y[None],
        input_grad[None],
        grad_w_qkv,
        grad_b_qkv,
        grad_w_out,
        vec[4],
        grad_w_up,
        grad_b_up,
        grad_w_down,
        vec[5],
        vec[0],
        vec[1],
        vec[2],
        vec[3],
        counts * (CLASSES / total_tokens),
    )


def solution(mesh):
    placed = (
        P(("dp", "tensor"), None, None),
        P("dp"),
        P(("dp", "tensor"), None),
        P(None, None, "tensor"),
        P(None, "tensor"),
        P("tensor", None),
        P(),
        P(None, "tensor"),
        P("tensor"),
        P("tensor", None),
        P(),
        P(),
        P(),
        P(),
        P(),
        P(("dp", "tensor"), None, None),
    )
    return jax.shard_map(
        per_device,
        mesh=mesh,
        in_specs=placed,
        out_specs=(
            P(("dp", "tensor"), None, None),
            P(("dp", "tensor"), None, None),
            P(None, None, "tensor"),
            P(None, "tensor"),
            P("tensor", None),
            P(),
            P(None, "tensor"),
            P("tensor"),
            P("tensor", None),
            P(),
            P(),
            P(),
            P(),
            P(),
            P(),
        ),
        check_vma=False,
    )
```

time: 925 us -> 452 us (0.49)
  matrix products: 257 us -> 0 us
  waiting for transfers between devices: 324 us -> 94.5 us
  Pallas kernels: 0 us -> 174 us
  other arithmetic: 154 us -> 22.7 us
  local copies, waits for them, and re-layouts: 44.4 us -> 11.7 us
    dot_general x26 -> x0, matrix products: 257 us -> none  [the longest x4 46.5 us: masked_scores(): jnp.einsum('qhd,khd->hqk', queries, keys_rot, preferred_element_type=jnp....]
    pallas_call x0 -> x14, Pallas kernels: none -> 174 us  [the longest x2 55.5 us: mlp(): call(functools.partial(mlp_body, last), (half // block,), in_specs, out_s...]
    psum x1, waiting for transfers between devices: 259 us -> 94.4 us  [total(): return lax.psum(own + swap(other), 'dp').astype(F32)]
    convert_element_type x15 -> x6, other arithmetic: 85.6 us -> 11.6 us  [the longest x4 9.68 us: total(): return lax.psum(own + swap(other), 'dp').astype(F32)]
    reduce_sum x14 -> x1, other arithmetic: 53.8 us -> 0.15 us  [per_device(): counts = jnp.sum(hits.astype(F32), axis=1)]
    all_gather x4 -> x0, waiting for transfers between devices: 39.6 us -> none  [the longest x1 13.7 us: per_device(): lax.all_gather(normed_one.astype(jnp.bfloat16), 'tensor', axis=0, tiled=T...]
    unnamed x116 -> x42, local copies, waits for them, and re-layouts: 28.5 us -> 3.66 us
    reduce_scatter x4 -> x0, waiting for transfers between devices: 24.8 us -> none  [the longest x1 12.4 us: per_device(): lax.psum_scatter(jnp.einsum('gle,ed->gld', picked, w_out, preferred_eleme...]
  transfers between devices with their start and end apart: 9 -> 13, of which waited for: 7 -> 1; matrix products, arithmetic and copies ran while one was open for 11% -> 4% of each run, Pallas kernels for 0% -> 34%
where the time goes in v1:
time: 452 us; the launch traced here: 443 us
  Pallas kernels  174 us (38%)
  blocking collectives  122 us (27%)
  waiting for transfers between devices  94.5 us (21%)
  other arithmetic  22.7 us (5%)
  between operations  14.5 us (3%)
  local copies, waits for them, and re-layouts  11.7 us (3%)
    psum x1, waiting for transfers between devices, total(): return lax.psum(own + swap(other), 'dp').astype(F32)  94.4 us
    psum x1, blocking collectives, total(): return lax.psum(own + swap(other), 'dp').astype(F32)  76.6 us
    pallas_call x2, Pallas kernels, mlp(): call(functools.partial(mlp_body, last), (half // block,), in_specs, out_s...  55.5 us
    psum x1, blocking collectives, per_device(): lax.psum((jnp.concatenate([vec1[:2], vec2[:4]]), counts), ('dp', 'tensor'))  45.2 us
    pallas_call x2, Pallas kernels, attend_grad(): call(attend_grad_body, (pairs,), [pl.BlockSpec((2, length, length), lambd...  33.7 us
    pallas_call x2, Pallas kernels, attend(): call(attend_body, (pairs,), [pl.BlockSpec(memory_space=pltpu.SMEM), col,...  31.9 us
    pallas_call x2, Pallas kernels, project(): call(functools.partial(project_body, normalize), (length // rows,), head_...  13.4 us
    pallas_call x2, Pallas kernels, weight_grad(): call(weight_grad_body, (1,), [full(n.shape)] + [full((length, half))] * 3...  11.8 us
  transfers between devices with their start and end apart: 13, of which 1 were waited for; matrix products, arithmetic and copies ran while one was open for 4% of the time, Pallas kernels for 34%

profile of v1, /device:TPU:0, one launch (start us, length us, event | category | flops | bytes accessed | tf_op | source)
XLA Modules:
  0.0 443.2 jit_solution(5990568697786434696)
XLA Ops:
  7.2 0.6 collective-permute-start.3
  8.4 0.4 collective-permute-start.4
  8.8 1.3 convert_element_type.14.refs_4_
  10.1 1.3 reshape.38.refs_1_.refs_10_
  11.3 1.3 reshape.39.refs_2_
  12.6 7.2 %project.2 = (bf16[1024,768]{1,0:T(8,128)(2,1)}, bf16[1024,384]{1,0:T(8,128)(2,1)}, bf16[1024,384]{1,0:T(8,128)(2,1)}, bf16[1024,384]{1,0:T(8,128)(2,1)}) custom-call(bf16[1024,768]{1,0:T(8,128)(2,1)} %bitcast.9, f32[1,768]{1,0:T(1,128)} %reshape.38.refs_1_.refs_10_, f32[1,768]{1,0:T(1,128)} %reshape.39.refs_2_, bf16[3,768,384]{2,1,0:T(8,128)(2,1)} %refs_6_.2, ...), custom_call_target="tpu_custom_call" | custom-call | flops 1811939328 | bytes 7274496 | tf_op jit(solution)/shard_map/project/pallas_call | solution.py:124
  19.8 0.6 dynamic_slice.3.len_ref
  20.5 16.0 %attend.2 = (bf16[6,1024,1024]{2,1,0:T(8,128)(2,1)}, bf16[384,1024]{1,0:T(8,128)(2,1)}, bf16[1024,384]{1,0:T(8,128)(2,1)}, f32[3,8,1024]{2,1,0:T(8,128)}) custom-call(s32[1]{0:T(128)} %dynamic_slice.3.len_ref, bf16[1024,384]{1,0:T(8,128)(2,1)} %get-tuple-element.60.q_ref, bf16[1024,384]{1,0:T(8,128)(2,1)} %get-tuple-element.61.k_ref, ...), custom_call_target="tpu_custom_call" | custom-call | flops 3221225472 | bytes 12582912 | tf_op jit(solution)/shard_map/attend/pallas_call | solution.py:180
  36.4 0.6 reshape.43.refs_3_
  37.0 0.6 reshape.41.g_ref.refs_9_
  37.6 0.6 reshape.40.b_ref
  38.2 0.6 reshape.45.refs_8_
  38.8 0.6 reshape.42.s_ref
  39.4 0.6 convert_element_type.15.refs_2_
  40.0 0.6 reshape.44.refs_3_
  40.6 6.2 %project.3 = (bf16[1024,384]{1,0:T(8,128)(2,1)}, bf16[1024,384]{1,0:T(8,128)(2,1)}, bf16[1024,384]{1,0:T(8,128)(2,1)}) custom-call(bf16[1024,768]{1,0:T(8,128)(2,1)} %get-tuple-element.64.refs_0_.n_ref, bf16[3,768,384]{2,1,0:T(8,128)(2,1)} %collective-permute-done.refs_1_.refs_7_, f32[3,384]{1,0:T(4,128)} %convert_element_type.15.refs_2_, ...), custom_call_target="tpu_custom_call" | custom-call | flops 1811939328 | bytes 7274496 | tf_op jit(solution)/shard_map/project/pallas_call | solution.py:124
  46.8 15.9 %attend.3 = (bf16[6,1024,1024]{2,1,0:T(8,128)(2,1)}, bf16[384,1024]{1,0:T(8,128)(2,1)}, bf16[1024,384]{1,0:T(8,128)(2,1)}, f32[3,8,1024]{2,1,0:T(8,128)}) custom-call(s32[1]{0:T(128)} %dynamic_slice.3.len_ref, bf16[1024,384]{1,0:T(8,128)(2,1)} %get-tuple-element.65.q_ref, bf16[1024,384]{1,0:T(8,128)(2,1)} %get-tuple-element.66.k_ref, ...), custom_call_target="tpu_custom_call" | custom-call | flops 3221225472 | bytes 12582912 | tf_op jit(solution)/shard_map/attend/pallas_call | solution.py:180
  62.7 0.8 copy-done.17
  63.5 6.3 %out_project.1 = (f32[1024,768]{1,0:T(8,128)}, bf16[1024,768]{1,0:T(8,128)(2,1)}) custom-call(bf16[1024,384]{1,0:T(8,128)(2,1)} %get-tuple-element.63.o1_ref, bf16[1024,384]{1,0:T(8,128)(2,1)} %get-tuple-element.68.o2_ref, bf16[384,768]{1,0:T(8,128)(2,1)} %w_ref.1, bf16[384,768]{1,0:T(8,128)(2,1)} %copy-done.17, bf16[1024,768]{1,0:T(8,128)(2,1)} %bitcast.10, ...), custom_call_target="tpu_custom_call" | custom-call | flops 1207959552 | bytes 7864320 | tf_op jit(solution)/shard_map/out_project/pallas_call | solution.py:290
  69.8 1.4 copy-done.15
  71.2 23.8 %mlp_first.1 = (bf16[768,1536]{1,0:T(8,128)(2,1)}, bf16[1536,768]{1,0:T(8,128)(2,1)}, f32[1,1536]{1,0:T(1,128)}, f32[1024,768]{1,0:T(8,128)}, f32[1024,768]{1,0:T(8,128)}) custom-call(bf16[1024,768]{1,0:T(8,128)(2,1)} %get-tuple-element.69.refs_0_, bf16[1024,768]{1,0:T(8,128)(2,1)} %bitcast.7, bf16[768,1536]{1,0:T(8,128)(2,1)} %copy-done.15, ...), custom_call_target="tpu_custom_call" | custom-call | flops 14495514624 | bytes 25165824 | tf_op jit(solution)/shard_map/mlp_first/pallas_call | solution.py:410
  95.1 0.5 collective-permute-start.9
  95.6 31.6 %mlp_last.1 = (bf16[768,1536]{1,0:T(8,128)(2,1)}, bf16[1536,768]{1,0:T(8,128)(2,1)}, f32[1,1536]{1,0:T(1,128)}, bf16[1024,768]{1,0:T(8,128)(2,1)}, f32[1024,768]...) custom-call(bf16[1024,768]{1,0:T(8,128)(2,1)} %get-tuple-element.69.refs_0_, bf16[1024,768]{1,0:T(8,128)(2,1)} %bitcast.8, ...), custom_call_target="tpu_custom_call" | custom-call | flops 14495514624 | bytes 25165824 | tf_op jit(solution)/shard_map/mlp_last/pallas_call | solution.py:410
  127.3 5.2 %mixed_grad.3 = (bf16[384,1024]{1,0:T(8,128)(2,1)}, bf16[384,768]{1,0:T(8,128)(2,1)}) custom-call(bf16[384,768]{1,0:T(8,128)(2,1)} %copy-done.17, bf16[384,1024]{1,0:T(8,128)(2,1)} %get-tuple-element.84.ot_ref, bf16[1024,768]{1,0:T(8,128)(2,1)} %get-tuple-element.77.ga_ref), custom_call_target="tpu_custom_call" | custom-call | flops 1207959552 | bytes 4325376 | tf_op jit(solution)/shard_map/mixed_grad/pallas_call | solution.py:434
  132.5 16.9 %attend_grad.3 = (bf16[1024,384]{1,0:T(8,128)(2,1)}, bf16[1024,384]{1,0:T(8,128)(2,1)}, bf16[1024,384]{1,0:T(8,128)(2,1)}) custom-call(bf16[6,1024,1024]{2,1,0:T(8,128)(2,1)} %get-tuple-element.82.e_ref, f32[3,8,1024]{2,1,0:T(8,128)} %get-tuple-element.83.linv_ref, bf16[1024,384]{1,0:T(8,128)(2,1)} %get-tuple-element.65.q_ref, ...), custom_call_target="tpu_custom_call" | custom-call | flops 6442450944 | bytes 12582912 | tf_op jit(solution)/shard_map/attend_grad/pallas_call | solution.py:255
  149.4 5.9 %weight_grad.3 = (bf16[3,768,384]{2,1,0:T(8,128)(2,1)}, f32[3,384]{1,0:T(4,128)}) custom-call(bf16[1024,768]{1,0:T(8,128)(2,1)} %get-tuple-element.64.refs_0_.n_ref, bf16[1024,384]{1,0:T(8,128)(2,1)} %get-tuple-element.86.refs_3_.dq_ref, bf16[1024,384]{1,0:T(8,128)(2,1)} %get-tuple-element.87.refs_4_.dk_ref, bf16[1024,384]{1,0:T(8,128)(2,1)} %get-tuple-element.88.refs_5_.dv_ref), custom_call_target="tpu_custom_call" | custom-call | flops 1811939328 | bytes 5701632 | tf_op jit(solution)/shard_map/weight_grad/pallas_call | solution.py:457
  155.9 5.2 %mixed_grad.2 = (bf16[384,1024]{1,0:T(8,128)(2,1)}, bf16[384,768]{1,0:T(8,128)(2,1)}) custom-call(bf16[384,768]{1,0:T(8,128)(2,1)} %w_ref.1, bf16[384,1024]{1,0:T(8,128)(2,1)} %get-tuple-element.76.ot_ref, bf16[1024,768]{1,0:T(8,128)(2,1)} %get-tuple-element.77.ga_ref), custom_call_target="tpu_custom_call" | custom-call | flops 1207959552 | bytes 4325376 | tf_op jit(solution)/shard_map/mixed_grad/pallas_call | solution.py:434
  161.1 16.8 %attend_grad.2 = (bf16[1024,384]{1,0:T(8,128)(2,1)}, bf16[1024,384]{1,0:T(8,128)(2,1)}, bf16[1024,384]{1,0:T(8,128)(2,1)}) custom-call(bf16[6,1024,1024]{2,1,0:T(8,128)(2,1)} %get-tuple-element.74.e_ref, f32[3,8,1024]{2,1,0:T(8,128)} %get-tuple-element.75.linv_ref, bf16[1024,384]{1,0:T(8,128)(2,1)} %get-tuple-element.60.q_ref, ...), custom_call_target="tpu_custom_call" | custom-call | flops 6442450944 | bytes 12582912 | tf_op jit(solution)/shard_map/attend_grad/pallas_call | solution.py:255
  177.9 5.9 %weight_grad.2 = (bf16[3,768,384]{2,1,0:T(8,128)(2,1)}, f32[3,384]{1,0:T(4,128)}) custom-call(bf16[1024,768]{1,0:T(8,128)(2,1)} %get-tuple-element.64.refs_0_.n_ref, bf16[1024,384]{1,0:T(8,128)(2,1)} %get-tuple-element.79.refs_0_.dq_ref, bf16[1024,384]{1,0:T(8,128)(2,1)} %get-tuple-element.80.refs_1_.dk_ref, bf16[1024,384]{1,0:T(8,128)(2,1)} %get-tuple-element.81.refs_2_.dv_ref), custom_call_target="tpu_custom_call" | custom-call | flops 1811939328 | bytes 5701632 | tf_op jit(solution)/shard_map/weight_grad/pallas_call | solution.py:457
  183.8 2.3 add.40
  186.1 1.7 add.38
  187.8 0.6 copy-done.3
  188.4 3.8 add.41
  192.2 2.0 add.43
  194.2 0.7 iota_compare_fusion.1
  195.1 0.5 collective-permute-start.10
  195.6 11.5 %input_grad.1 = (bf16[1024,768]{1,0:T(8,128)(2,1)}, f32[8,768]{1,0:T(8,128)}) custom-call(bf16[1024,384]{1,0:T(8,128)(2,1)} %get-tuple-element.79.refs_0_.dq_ref, bf16[1024,384]{1,0:T(8,128)(2,1)} %get-tuple-element.80.refs_1_.dk_ref, bf16[1024,384]{1,0:T(8,128)(2,1)} %get-tuple-element.81.refs_2_.dv_ref, ...), custom_call_target="tpu_custom_call" | custom-call | flops 3623878656 | bytes 15728640 | tf_op jit(solution)/shard_map/input_grad/pallas_call | solution.py:496
  207.1 0.7 slice.24
  208.1 45.2 %all-reduce = (f32[6,768]{1,0:T(8,128)S(1)}, f32[70]{0:T(128)S(1)}) all-reduce(f32[6,768]{1,0:T(8,128)S(1)} %pad_maximum_fusion, f32[70]{0:T(128)S(1)} %convert_reduce_fusion), channel_id=1, replica_groups=mesh['dp'=16,'tensor'=2] {'dp','tensor'}, use_global_device_ids=true, to_apply=%region_3.0 | all-reduce | flops 4678 | bytes 37424 | tf_op jit(solution)/shard_map/psum | solution.py:572
  253.4 0.5 broadcast_multiply_fusion
  253.9 0.6 slice_reduce_fusion
  254.6 76.6 %all-reduce.1 = (f32[3,384]{1,0:T(4,128)}, f32[1536]{0:T(1024)}) all-reduce(f32[3,384]{1,0:T(4,128)S(1)} %add.39, f32[1536]{0:T(1024)S(1)} %add_reduce_fusion), channel_id=1, replica_groups=mesh['dp'=16,'tensor'=2] {'dp'}, use_global_device_ids=true, to_apply=%region_1.0 | all-reduce | flops 2688 | bytes 21504 | tf_op jit(solution)/shard_map/psum | solution.py:559
  331.2 94.4 %all-reduce.5.cloned.1.call-done = (bf16[3,768,384]{2,1,0:T(8,128)(2,1)}, bf16[384,768]{1,0:T(8,128)(2,1)}, bf16[768,1536]{1,0:T(8,128)(2,1)}, bf16[1536,768]{1,0:T(8,128)(2,1)}) async-done(((bf16[3,768,384]{2,1,0:T(8,128)(2,1)}, bf16[384,768]{1,0:T(8,128)(2,1)}, bf16[768,1536]{1,0:T(8,128)(2,1)}, bf16[1536,768]{1,0:T(8,128)(2,1)}), (bf16[3,768,384]{2,1,0:T(8,128)(2,1)}, bf16[384,768]{1,0:T(8,128)(2,1)}, ...) | async-done | bytes 7077904 | tf_op jit(solution)/shard_map/psum | solution.py:559
  425.6 2.3 convert_element_type.34
  427.9 2.0 convert_element_type.16
  430.0 0.8 copy-done.2
  430.8 2.8 convert_element_type.35
  433.6 2.5 convert_element_type.36
  (65 shorter events, 1.9 us)
Async XLA Ops:
  7.2 418.5 %all-reduce.5.cloned.1.call-start = ((), (), s32[]{:S(2)}) async-start(), calls=%async_computation | async-start | bytes 14155776 | tf_op jit(solution)/shard_map/psum | solution.py:559
  7.2 62.6 %collective-permute-start.3 = (bf16[768,1536]{1,0:T(8,128)(2,1)}, bf16[768,1536]{1,0:T(8,128)(2,1)S(1)}, u32[]{:S(2)}, u32[]{:S(2)}) collective-permute-start(bf16[768,1536]{1,0:T(8,128)(2,1)} %refs_2_.1), channel_id=1, source_target_pairs={{0,1},{1,0},{2,3},{3,2},{4,5},{5,4},{6,7},{7,6},{8,9},{9,8},{10,11... | collective-permute-start | bytes 7077896 | tf_op jit(solution)/shard_map/ppermute | solution.py:528
  7.8 62.0 %collective-permute-start.5 = (bf16[1536,768]{1,0:T(8,128)(2,1)}, bf16[1536,768]{1,0:T(8,128)(2,1)}, u32[]{:S(2)}, u32[]{:S(2)}) collective-permute-start(bf16[1536,768]{1,0:T(8,128)(2,1)} %refs_4_.2), channel_id=1, source_target_pairs={{0,1},{1,0},{2,3},{3,2},{4,5},{5,4},{6,7},{7,6},{8,9},{9,8},{10,11... | collective-permute-start | bytes 7077896 | tf_op jit(solution)/shard_map/ppermute | solution.py:528
  7.9 32.7 %collective-permute-start = (bf16[3,768,384]{2,1,0:T(8,128)(2,1)}, bf16[3,768,384]{2,1,0:T(8,128)(2,1)}, u32[]{:S(2)}, u32[]{:S(2)}) collective-permute-start(bf16[3,768,384]{2,1,0:T(8,128)(2,1)} %refs_6_.2), channel_id=1, source_target_pairs={{0,1},{1,0},{2,3},{3,2},{4,5},{5,4},{6,7},{7,6},{8,9},{9,8},{10,11... | collective-permute-start | bytes 5308424 | tf_op jit(solution)/shard_map/ppermute | solution.py:528
  8.3 12.1 %collective-permute-start.1 = (bf16[3,384]{1,0:T(4,128)(2,1)}, bf16[3,384]{1,0:T(4,128)(2,1)S(1)}, u32[]{:S(2)}, u32[]{:S(2)}) collective-permute-start(bf16[3,384]{1,0:T(4,128)(2,1)} %param.22), channel_id=1, source_target_pairs={{0,1},{1,0},{2,3},{3,2},{4,5},{5,4},{6,7},{7,6},{8,9},{9,8},{10,11... | collective-permute-start | bytes 6920 | tf_op jit(solution)/shard_map/ppermute | solution.py:528
  8.4 31.6 %collective-permute-start.4 = (bf16[1536]{0:T(1024)(128)(2,1)}, bf16[1536]{0:T(1024)(128)(2,1)S(1)}, u32[]{:S(2)}, u32[]{:S(2)}) collective-permute-start(bf16[1536]{0:T(1024)(128)(2,1)} %param.26), channel_id=1, source_target_pairs={{0,1},{1,0},{2,3},{3,2},{4,5},{5,4},{6,7},{7,6},{8,9},{9,8},{10,11... | collective-permute-start | bytes 9224 | tf_op jit(solution)/shard_map/ppermute | solution.py:528
  12.6 7.2 %copy-start.20 = (s32[2]{0:T(128)S(1)}, s32[2]{0:T(128)}, u32[]{:S(2)}) copy-start(s32[2]{0:T(128)} %param.19) | copy-start | bytes 28
  12.6 7.8 %copy-start.16 = (bf16[384,768]{1,0:T(8,128)(2,1)S(1)}, bf16[384,768]{1,0:T(8,128)(2,1)}, u32[]{:S(2)}) copy-start(bf16[384,768]{1,0:T(8,128)(2,1)} %w_ref.1) | copy-start | bytes 1769476
  20.4 42.3 %collective-permute-start.2 = (bf16[384,768]{1,0:T(8,128)(2,1)S(1)}, bf16[384,768]{1,0:T(8,128)(2,1)S(1)}, u32[]{:S(2)}, u32[]{:S(2)}) collective-permute-start(bf16[384,768]{1,0:T(8,128)(2,1)S(1)} %copy-done.16), channel_id=1, source_target_pairs={{0,1},{1,0},{2,3},{3,2},{4,5},{5,4},{6,7},{7,6},{8,9},{9,8},{10,11... | collective-permute-start | bytes 1769480 | tf_op jit(solution)/shard_map/ppermute | solution.py:528
  20.4 16.0 %copy-start.9 = (bf16[1536]{0:T(1024)(128)(2,1)S(1)}, bf16[1536]{0:T(1024)(128)(2,1)}, u32[]{:S(2)}) copy-start(bf16[1536]{0:T(1024)(128)(2,1)} %param.26) | copy-start | bytes 9220
  20.5 16.6 %copy-start.11 = (bf16[768]{0:T(1024)(128)(2,1)S(1)}, bf16[768]{0:T(1024)(128)(2,1)}, u32[]{:S(2)}) copy-start(bf16[768]{0:T(1024)(128)(2,1)} %param.31) | copy-start | bytes 4612
  20.5 17.2 %copy-start.12 = (bf16[768]{0:T(1024)(128)(2,1)S(1)}, bf16[768]{0:T(1024)(128)(2,1)}, u32[]{:S(2)}) copy-start(bf16[768]{0:T(1024)(128)(2,1)} %param.24) | copy-start | bytes 4612
  20.5 17.8 %copy-start.13 = (bf16[768]{0:T(1024)(128)(2,1)S(1)}, bf16[768]{0:T(1024)(128)(2,1)}, u32[]{:S(2)}) copy-start(bf16[768]{0:T(1024)(128)(2,1)} %param.28) | copy-start | bytes 4612
  20.5 18.3 %copy-start.14 = (bf16[768]{0:T(1024)(128)(2,1)S(1)}, bf16[768]{0:T(1024)(128)(2,1)}, u32[]{:S(2)}) copy-start(bf16[768]{0:T(1024)(128)(2,1)} %param.32) | copy-start | bytes 4612
  62.7 0.8 copy-start.17
  69.8 1.4 copy-start.15
  95.1 92.8 %collective-permute-start.9 = (bf16[768,1536]{1,0:T(8,128)(2,1)}, bf16[768,1536]{1,0:T(8,128)(2,1)}, u32[]{:S(2)}, u32[]{:S(2)}) collective-permute-start(bf16[768,1536]{1,0:T(8,128)(2,1)} %get-tuple-element.100), channel_id=1, source_target_pairs={{0,1},{1,0},{2,3},{3,2},{4,5},{5,4},{6,7},{7,6},{8,9},{9,8},{10,11... | collective-permute-start | bytes 7077896 | tf_op jit(solution)/shard_map/ppermute | solution.py:528
  95.6 96.6 %collective-permute-start.11 = (bf16[1536,768]{1,0:T(8,128)(2,1)}, bf16[1536,768]{1,0:T(8,128)(2,1)S(1)}, u32[]{:S(2)}, u32[]{:S(2)}) collective-permute-start(bf16[1536,768]{1,0:T(8,128)(2,1)} %get-tuple-element.104), channel_id=1, source_target_pairs={{0,1},{1,0},{2,3},{3,2},{4,5},{5,4},{6,7},{7,6},{8,9},{9,8},{10,11... | collective-permute-start | bytes 7077896 | tf_op jit(solution)/shard_map/ppermute | solution.py:528
  155.4 30.8 %collective-permute-start.6 = (bf16[3,768,384]{2,1,0:T(8,128)(2,1)}, bf16[3,768,384]{2,1,0:T(8,128)(2,1)S(1)}, u32[]{:S(2)}, u32[]{:S(2)}) collective-permute-start(bf16[3,768,384]{2,1,0:T(8,128)(2,1)} %get-tuple-element.92), channel_id=1, source_target_pairs={{0,1},{1,0},{2,3},{3,2},{4,5},{5,4},{6,7},{7,6},{8,9},{9,8},{10,11... | collective-permute-start | bytes 5308424 | tf_op jit(solution)/shard_map/ppermute | solution.py:528
  155.8 28.0 %collective-permute-start.8 = (bf16[384,768]{1,0:T(8,128)(2,1)}, bf16[384,768]{1,0:T(8,128)(2,1)}, u32[]{:S(2)}, u32[]{:S(2)}) collective-permute-start(bf16[384,768]{1,0:T(8,128)(2,1)} %get-tuple-element.96), channel_id=1, source_target_pairs={{0,1},{1,0},{2,3},{3,2},{4,5},{5,4},{6,7},{7,6},{8,9},{9,8},{10,11... | collective-permute-start | bytes 1769480 | tf_op jit(solution)/shard_map/ppermute | solution.py:528
  183.8 2.3 copy-start.5
  186.1 2.2 copy-start.3
  188.4 3.8 copy-start
  194.2 0.7 copy-start.10
  194.2 0.9 copy-start.18
  194.2 1.4 copy-start.6
  195.1 59.5 %collective-permute-start.10 = (f32[1,1536]{1,0:T(1,128)S(1)}, f32[1,1536]{1,0:T(1,128)S(1)}, u32[]{:S(2)}, u32[]{:S(2)}) collective-permute-start(f32[1,1536]{1,0:T(1,128)S(1)} %copy-done.18), channel_id=1, source_target_pairs={{0,1},{1,0},{2,3},{3,2},{4,5},{5,4},{6,7},{7,6},{8,9},{9,8},{10,11... | collective-permute-start | bytes 18440 | tf_op jit(solution)/shard_map/ppermute | solution.py:528
  195.6 12.3 %copy-start.19 = (f32[3,384]{1,0:T(4,128)S(1)}, f32[3,384]{1,0:T(4,128)}, u32[]{:S(2)}) copy-start(f32[3,384]{1,0:T(4,128)} %get-tuple-element.94) | copy-start | bytes 13828
  195.6 59.0 %copy-start.8 = (f32[3,384]{1,0:T(4,128)S(1)}, f32[3,384]{1,0:T(4,128)}, u32[]{:S(2)}) copy-start(f32[3,384]{1,0:T(4,128)} %get-tuple-element.93) | copy-start | bytes 13828
  195.6 59.0 %copy-start.7 = (f32[1,1536]{1,0:T(1,128)S(1)}, f32[1,1536]{1,0:T(1,128)}, u32[]{:S(2)}) copy-start(f32[1,1536]{1,0:T(1,128)} %get-tuple-element.101) | copy-start | bytes 18436
  207.8 46.7 %collective-permute-start.7 = (f32[3,384]{1,0:T(4,128)S(1)}, f32[3,384]{1,0:T(4,128)S(1)}, u32[]{:S(2)}, u32[]{:S(2)}) collective-permute-start(f32[3,384]{1,0:T(4,128)S(1)} %copy-done.19), channel_id=1, source_target_pairs={{0,1},{1,0},{2,3},{3,2},{4,5},{5,4},{6,7},{7,6},{8,9},{9,8},{10,11... | collective-permute-start | bytes 13832 | tf_op jit(solution)/shard_map/ppermute | solution.py:528
  425.6 2.3 copy-start.4
  427.9 2.8 copy-start.2
  430.8 2.8 copy-start.1
Sparse Core Ops, SparseCore 0:
  194.3 231.2 all-reduce.4
